TPU v7x, 32 devices: a whole 2x2x4 slice. The times are simulated.
32 devices in a mesh: ctx: 8 (over z, x), heads: 4 (over y, core).
Axes of the slice: x: 2, y: 2, z: 4, core: 2. Of those that a mesh axis runs over, the one named last changes fastest.
Arguments:
- activations: bfloat16 [2048, 8192], P('ctx', 'heads'), may hold values from -20 to 20
- w_query: bfloat16 [8192, 4096], P(None, 'heads'), may hold values from -0.0625 to 0.0625
- w_key: bfloat16 [8192, 1024], P(None, 'heads'), may hold values from -0.0625 to 0.0625
- w_value: bfloat16 [8192, 1024], P(None, 'heads'), may hold values from -0.0625 to 0.0625
- doc_lengths: int32 [8], replicated, may hold values from 1 to 1024, 2048 in all
- block_dest: int32 [32], replicated, may hold values from 0 to 7, as said below
- out_grad: bfloat16 [2048, 4096], P('ctx', 'heads'), may hold values from -6 to 6
Outputs:
- attention: bfloat16 [2048, 4096], P('ctx', 'heads')
- input_grad: bfloat16 [2048, 8192], P('ctx', 'heads')
Inputs may be any that keep to these rules, and one draw needn't show every extreme that they name: `block_dest`: loader block b lies on loader shard b // 4. Each loader shard sends its blocks to different context shards, and each context shard receives exactly 4 blocks, from different loader shards.
All inputs are finite; a program needn't handle non-finite values.
Results may differ from a plain program's by a relative error of at most 0.025.
The roundings to bfloat16 on the way count: a program that leaves them out, or rounds other values in their place, can miss the bound.
Values may be sent and summed in bfloat16 or wider, within the bound.
A program may use at most 128 MiB of HBM per device.

v0:
```python
import math
import jax
import jax.numpy as jnp
from jax import lax
from jax.sharding import PartitionSpec as P

HD = 128
QPK = 4
NEG = -1e30


def from_behind(value, axis, steps):
    count = lax.axis_size(axis)
    pairs = [(source, (source + steps) % count) for source in range(count)]
    return lax.ppermute(value, axis, pairs)


def layout(block_dest, block_rows):
    nblk = block_dest.shape[0]
    index = jnp.arange(nblk, dtype=jnp.int32)
    order_key = block_dest * nblk + index
    ranks = jnp.sum((order_key[None, :] < order_key[:, None]).astype(jnp.int32), axis=1)
    ctx_blocks = jnp.sum(jnp.where(ranks[None, :] == index[:, None], index[None, :], 0), axis=1)
    ctx_pos = (
        ctx_blocks[:, None] * block_rows + jnp.arange(block_rows, dtype=jnp.int32)[None, :]
    ).reshape(-1)
    return (ctx_blocks, ctx_pos)


def doc_ids(positions, doc_lengths):
    ends = jnp.cumsum(doc_lengths)
    return jnp.sum((ends[None, :] <= positions[:, None]).astype(jnp.int32), axis=1)


def spread(table, array, block_rows):
    width = array.shape[-1]
    grouped = array.reshape(table.shape[1], block_rows, width)
    moved = jnp.einsum("ab,brf->arf", table, grouped, preferred_element_type=jnp.float32)
    return moved.astype(jnp.bfloat16)


def transposed_dot(left, weight):
    return lax.dot_general(
        left, weight, (((1,), (1,)), ((), ())), preferred_element_type=jnp.float32
    )


def per_device(activations, w_query, w_key, w_value, doc_lengths, block_dest, out_grad):
    ctx_count = lax.axis_size("ctx")
    ctx_rank = lax.axis_index("ctx")
    tok_dev = activations.shape[0]
    block_rows = tok_dev * ctx_count // block_dest.shape[0]
    blocks_here = tok_dev // block_rows
    head_dim = HD
    groups = w_key.shape[1] // head_dim
    per_group = QPK
    scale = 1.0 / math.sqrt(head_dim)
    ctx_blocks, ctx_pos = layout(block_dest, block_rows)
    ctx_doc = doc_ids(ctx_pos, doc_lengths)
    my_pos = lax.dynamic_slice_in_dim(ctx_pos, ctx_rank * tok_dev, tok_dev, 0)
    my_doc = lax.dynamic_slice_in_dim(ctx_doc, ctx_rank * tok_dev, tok_dev, 0)
    piece = lax.all_gather(activations, "heads", axis=1, tiled=True)
    rows = piece.shape[1]
    proj_q = jnp.dot(piece, w_query, preferred_element_type=jnp.float32)
    proj_k = jnp.dot(piece, w_key, preferred_element_type=jnp.float32)
    proj_v = jnp.dot(piece, w_value, preferred_element_type=jnp.float32)
    loader_q = proj_q.astype(jnp.bfloat16)
    loader_k = proj_k.astype(jnp.bfloat16)
    loader_v = proj_v.astype(jnp.bfloat16)
    slots = jnp.arange(ctx_count, dtype=jnp.int32)
    my_dest = lax.dynamic_slice_in_dim(block_dest, ctx_rank * blocks_here, blocks_here, 0)
    send_map = (my_dest[None, :] == slots[:, None]).astype(jnp.bfloat16)
    mine = lax.dynamic_slice_in_dim(ctx_blocks, ctx_rank * blocks_here, blocks_here, 0)
    source = mine // blocks_here
    take_map = (source[:, None] == slots[None, :]).astype(jnp.bfloat16)
    recv_q, recv_k, recv_v = (
        lax.all_to_all(
            spread(send_map, loader_q, block_rows), "ctx", split_axis=0, concat_axis=0, tiled=True
        ),
        lax.all_to_all(
            spread(send_map, loader_k, block_rows), "ctx", split_axis=0, concat_axis=0, tiled=True
        ),
        lax.all_to_all(
            spread(send_map, loader_v, block_rows), "ctx", split_axis=0, concat_axis=0, tiled=True
        ),
    )
    ctx_q = spread(take_map, recv_q.reshape(ctx_count * block_rows, -1), block_rows).reshape(
        tok_dev, -1
    )
    ctx_k = spread(take_map, recv_k.reshape(ctx_count * block_rows, -1), block_rows).reshape(
        tok_dev, -1
    )
    ctx_v = spread(take_map, recv_v.reshape(ctx_count * block_rows, -1), block_rows).reshape(
        tok_dev, -1
    )
    query_four = ctx_q.reshape(tok_dev, groups, per_group, head_dim)

    def visible(key_pos, key_doc):
        return (my_doc[:, None] == key_doc[None, :]) & (key_pos[None, :] <= my_pos[:, None])

    def attend(state, key_blk, value_blk, key_pos, key_doc):
        mask = visible(key_pos, key_doc)

        def attend_run(inner):
            m_old, l_old, accum = inner
            scores = (
                jnp.einsum(
                    "tgqe,sge->gqts", query_four, key_blk, preferred_element_type=jnp.float32
                )
                * scale
            )
            scores = jnp.where(mask[None, None], scores, NEG)
            m_new = jnp.maximum(m_old, jnp.max(scores, axis=-1))
            factor = jnp.exp(m_old - m_new)
            probs = jnp.where(mask[None, None], jnp.exp(scores - m_new[..., None]), 0.0)
            l_new = l_old * factor + jnp.sum(probs, axis=-1)
            accum = accum * factor[..., None] + jnp.einsum(
                "gqts,sge->gqte",
                probs,
                value_blk.astype(jnp.float32),
                precision=lax.Precision.HIGHEST,
                preferred_element_type=jnp.float32,
            )
            return (m_new, l_new, accum)

        return lax.cond(jnp.any(mask), attend_run, lambda inner: inner, state)

    start_state = (
        jnp.full((groups, per_group, tok_dev), NEG, jnp.float32),
        jnp.zeros((groups, per_group, tok_dev), jnp.float32),
        jnp.zeros((groups, per_group, tok_dev, head_dim), jnp.float32),
    )
    grad_four = out_grad.reshape(tok_dev, groups, per_group, head_dim)

    def grads_over(dquery, key_piece, value_piece, start, lse, delta):
        rows = key_piece.shape[0]
        width = math.gcd(rows, 512)

        def grads_one_block(index, inner):
            dq_sum, dk_rows, dv_rows = inner
            offset = index * width
            key_blk = key_piece.reshape(width, groups, head_dim)
            value_blk = value_piece.reshape(width, groups, head_dim)
            key_pos = lax.dynamic_slice_in_dim(ctx_pos, start + offset, width, 0)
            key_doc = lax.dynamic_slice_in_dim(ctx_doc, start + offset, width, 0)
            mask = visible(key_pos, key_doc)

            def one_run(unused):
                scores = (
                    jnp.einsum(
                        "tgqe,sge->gqts", query_four, key_blk, preferred_element_type=jnp.float32
                    )
                    * scale
                )
                weights = jnp.where(mask[None, None], jnp.exp(scores - lse[..., None]), 0.0)
                weights_b = weights.astype(jnp.bfloat16)
                dv_blk = jnp.einsum(
                    "gqts,tgqe->sge", weights_b, grad_four, preferred_element_type=jnp.float32
                )
                dprob = jnp.einsum(
                    "tgqe,sge->gqts", grad_four, value_blk, preferred_element_type=jnp.float32
                )
                dscore = (weights * (dprob - delta[..., None]) * scale).astype(jnp.bfloat16)
                dq_add = jnp.einsum(
                    "gqts,sge->tgqe", dscore, key_blk, preferred_element_type=jnp.float32
                )
                dk_blk = jnp.einsum(
                    "gqts,tgqe->sge", dscore, query_four, preferred_element_type=jnp.float32
                )
                return (dq_add, dk_blk, dv_blk)

            def skip(unused):
                return (
                    jnp.zeros((tok_dev, groups, per_group, head_dim), jnp.float32),
                    jnp.zeros((width, groups, head_dim), jnp.float32),
                    jnp.zeros((width, groups, head_dim), jnp.float32),
                )

            dq_add, dk_blk, dv_blk = lax.cond(jnp.any(mask), one_run, skip, 0)
            dk_rows = dk_blk.reshape(width, groups * head_dim)
            dv_rows = dv_blk.reshape(width, groups * head_dim)
            return (dq_sum + dq_add, dk_rows, dv_rows)

        empty_rows = jnp.zeros((rows, groups * head_dim), jnp.float32)
        return lax.fori_loop(0, rows // width, grads_one_block, (dquery, empty_rows, empty_rows))

    dq_start = jnp.zeros((tok_dev, groups, per_group, head_dim), jnp.float32)
    key_piece = lax.all_gather(ctx_k, "ctx", axis=0, tiled=True)
    value_piece = lax.all_gather(ctx_v, "ctx", axis=0, tiled=True)
    rows = key_piece.shape[0]
    width = math.gcd(rows, 512)

    def fold_one_block(index, inner):
        offset = index * width
        key_blk = lax.dynamic_slice_in_dim(key_piece, offset, width, 0).reshape(
            width, groups, head_dim
        )
        value_blk = lax.dynamic_slice_in_dim(value_piece, offset, width, 0).reshape(
            width, groups, head_dim
        )
        key_pos = lax.dynamic_slice_in_dim(ctx_pos, offset, width, 0)
        key_doc = lax.dynamic_slice_in_dim(ctx_doc, offset, width, 0)
        return attend(inner, key_blk, value_blk, key_pos, key_doc)

    m_end, l_end, accum = lax.fori_loop(0, rows // width, fold_one_block, start_state)
    attn = (accum / l_end[..., None]).astype(jnp.bfloat16)
    attention = attn.transpose(2, 0, 1, 3).reshape(tok_dev, groups * per_group * head_dim)
    lse = m_end + jnp.log(l_end)
    attn_four = attention.reshape(tok_dev, groups, per_group, head_dim)
    delta = jnp.einsum(
        "tgqe,tgqe->gqt", grad_four.astype(jnp.float32), attn_four.astype(jnp.float32)
    )

    def turn(step, inner):
        dquery, key_now, value_now, dk_now, dv_now = inner
        owner = jnp.mod(ctx_rank - step, ctx_count)
        dquery, dk_add, dv_add = grads_over(dquery, key_now, value_now, owner * tok_dev, lse, delta)
        dk_now, dv_now = (
            from_behind((dk_now + dk_add).astype(jnp.bfloat16), "ctx", 1).astype(jnp.float32),
            from_behind((dv_now + dv_add).astype(jnp.bfloat16), "ctx", 1).astype(jnp.float32),
        )
        key_now, value_now = from_behind((key_now, value_now), "ctx", 1)
        return (dquery, key_now, value_now, dk_now, dv_now)

    zero_grads = jnp.zeros((tok_dev, groups * head_dim), jnp.float32)
    dquery, unused_k, unused_v, dkey, dvalue = lax.fori_loop(
        0, ctx_count, turn, (dq_start, ctx_k, ctx_v, zero_grads, zero_grads)
    )
    dq_ctx = dquery.reshape(tok_dev, groups * per_group * head_dim).astype(jnp.bfloat16)
    dk_ctx = dkey.astype(jnp.bfloat16)
    dv_ctx = dvalue.astype(jnp.bfloat16)
    back_map = take_map.T
    home_q, home_k, home_v = (
        lax.all_to_all(
            spread(back_map, dq_ctx, block_rows), "ctx", split_axis=0, concat_axis=0, tiled=True
        ),
        lax.all_to_all(
            spread(back_map, dk_ctx, block_rows), "ctx", split_axis=0, concat_axis=0, tiled=True
        ),
        lax.all_to_all(
            spread(back_map, dv_ctx, block_rows), "ctx", split_axis=0, concat_axis=0, tiled=True
        ),
    )
    pick_map = send_map.T
    dq_loader = spread(pick_map, home_q.reshape(ctx_count * block_rows, -1), block_rows).reshape(
        tok_dev, -1
    )
    dk_loader = spread(pick_map, home_k.reshape(ctx_count * block_rows, -1), block_rows).reshape(
        tok_dev, -1
    )
    dv_loader = spread(pick_map, home_v.reshape(ctx_count * block_rows, -1), block_rows).reshape(
        tok_dev, -1
    )
    grad_terms = (
        transposed_dot(dq_loader, w_query)
        + transposed_dot(dk_loader, w_key)
        + transposed_dot(dv_loader, w_value)
    )
    input_grad = lax.psum_scatter(
        grad_terms.astype(jnp.bfloat16), "heads", scatter_dimension=1, tiled=True
    )
    return (attention, input_grad)


def solution(mesh):
    return jax.shard_map(
        per_device,
        mesh=mesh,
        in_specs=(
            P("ctx", "heads"),
            P(None, "heads"),
            P(None, "heads"),
            P(None, "heads"),
            P(),
            P(),
            P("ctx", "heads"),
        ),
        out_specs=(P("ctx", "heads"), P("ctx", "heads")),
        check_vma=False,
    )
```

profile of v0, /device:TPU:0, one launch (start us, length us, event | category | flops | bytes accessed | tf_op | source)
XLA Modules:
  0.0 553.3 jit_solution(3324979120740839685)
XLA Ops:
  9.7 37.1 %all-gather.4.cloned.1.call-done = bf16[256,8192]{1,0:T(8,128)(2,1)} async-done(((bf16[256,2048]{1,0:T(8,128)(2,1)}), bf16[256,8192]{1,0:T(8,128)(2,1)}) %all-gather.4.cloned.1.call-update) | async-done | bytes 4194320 | tf_op jit(solution)/shard_map/all_gather | solution.py:62
  46.8 4.7 convolution_convert_fusion.13
  52.6 5.5 all-to-all-start.2
  58.1 4.7 convolution_convert_fusion.14
  63.9 3.5 all-to-all-done.2
  67.4 3.6 all-to-all-start
  72.1 11.5 %convolution_convert_fusion.4 = bf16[256,1024]{1,0:T(8,128)(2,1)S(1)} fusion(bf16[256,8192]{1,0:T(8,128)(2,1)} %all-gather.4.cloned.1.call-done, bf16[8192,1024]{1,0:T(8,128)(2,1)} %param.16), kind=kOutput, calls=%fused_computation.45 | convolution fusion | flops 4295229440 | bytes 21495808 | tf_op jit(solution)/shard_map/dot_general | solution.py:64
  85.8 6.0 %all-to-all-start.1 = ((bf16[8,64,1024]{2,1,0:T(8,128)(2,1)}), bf16[8,64,1024]{2,1,0:T(8,128)(2,1)S(1)}, u32[]{:S(2)}, u32[]{:S(2)}) async-start(bf16[8,64,1024]{2,1,0:T(8,128)(2,1)} %copy.107), calls=%async_computation.1 | async-start | bytes 2097152 | tf_op jit(solution)/shard_map/all_to_all | solution.py:77
  98.1 27.5 %all-to-all-done.1 = bf16[8,64,1024]{2,1,0:T(8,128)(2,1)S(1)} async-done(((bf16[8,64,1024]{2,1,0:T(8,128)(2,1)}), bf16[8,64,1024]{2,1,0:T(8,128)(2,1)S(1)}, u32[]{:S(2)}, u32[]{:S(2)}) %all-to-all-start.1) | async-done | bytes 1048608 | tf_op jit(solution)/shard_map/all_to_all | solution.py:77
  129.8 36.9 %all-gather.6.cloned.1.call-done = bf16[2048,256]{1,0:T(8,128)(2,1)} async-done(((bf16[256,256]{1,0:T(8,128)(2,1)}), bf16[2048,256]{1,0:T(8,128)(2,1)}) %all-gather.6.cloned.1.call-update) | async-done | bytes 1048592 | tf_op jit(solution)/shard_map/all_gather | solution.py:188
  170.0 47.4 %while.56 = (s32[]{:T(128)}, f32[2,4,256]{2,1,0:T(4,128)S(1)}, f32[2,4,256]{2,1,0:T(4,128)S(1)}, f32[2,4,256,128]{3,2,1,0:T(8,128)}, s32[256]{0:T(256)}, /*index...) while((s32[]{:T(128)}, f32[2,4,256]{2,1,0:T(4,128)S(1)}, ...), condition=%wide.region_10.11_spmd, body=%wide.region_4.10_spmd.sunk | while | flops 1892683776 | bytes 25835900 | solution.py:205
  173.7 8.2 %conditional.5 = ((f32[2,4,256]{2,1,0:T(4,128)S(1)}, f32[2,4,256]{2,1,0:T(4,128)S(1)}, f32[2,4,256,128]{3,2,1,0:T(8,128)})) conditional(s32[]{:T(128)} %convert_element_type.201, (f32[2,4,256]{2,1,0:T(4,128)S(1)}, f32[2,4,256]{2,1,0:T(4,128)S(1)}, f32[2,4,256,128]{3,2,1,0:T(8,128)}) %tuple.116, (pred[256,512]{0,1:T(8,128)(4,1)S(1)}, ...), branch_computations={%region_6.6_spmd, %region_7.9_spmd} | conditional | flops 1892159488 | bytes 25690204 | solution.py:126
  176.6 4.2 fusion.8
  185.5 8.2 %conditional.5 = ((f32[2,4,256]{2,1,0:T(4,128)S(1)}, f32[2,4,256]{2,1,0:T(4,128)S(1)}, f32[2,4,256,128]{3,2,1,0:T(8,128)})) conditional(s32[]{:T(128)} %convert_element_type.201, (f32[2,4,256]{2,1,0:T(4,128)S(1)}, f32[2,4,256]{2,1,0:T(4,128)S(1)}, f32[2,4,256,128]{3,2,1,0:T(8,128)}) %tuple.116, (pred[256,512]{0,1:T(8,128)(4,1)S(1)}, ...), branch_computations={%region_6.6_spmd, %region_7.9_spmd} | conditional | flops 1892159488 | bytes 25690204 | solution.py:126
  188.5 4.2 fusion.8
  197.4 8.2 %conditional.5 = ((f32[2,4,256]{2,1,0:T(4,128)S(1)}, f32[2,4,256]{2,1,0:T(4,128)S(1)}, f32[2,4,256,128]{3,2,1,0:T(8,128)})) conditional(s32[]{:T(128)} %convert_element_type.201, (f32[2,4,256]{2,1,0:T(4,128)S(1)}, f32[2,4,256]{2,1,0:T(4,128)S(1)}, f32[2,4,256,128]{3,2,1,0:T(8,128)}) %tuple.116, (pred[256,512]{0,1:T(8,128)(4,1)S(1)}, ...), branch_computations={%region_6.6_spmd, %region_7.9_spmd} | conditional | flops 1892159488 | bytes 25690204 | solution.py:126
  200.4 4.2 fusion.8
  209.2 8.2 %conditional.5 = ((f32[2,4,256]{2,1,0:T(4,128)S(1)}, f32[2,4,256]{2,1,0:T(4,128)S(1)}, f32[2,4,256,128]{3,2,1,0:T(8,128)})) conditional(s32[]{:T(128)} %convert_element_type.201, (f32[2,4,256]{2,1,0:T(4,128)S(1)}, f32[2,4,256]{2,1,0:T(4,128)S(1)}, f32[2,4,256,128]{3,2,1,0:T(8,128)}) %tuple.116, (pred[256,512]{0,1:T(8,128)(4,1)S(1)}, ...), branch_computations={%region_6.6_spmd, %region_7.9_spmd} | conditional | flops 1892159488 | bytes 25690204 | solution.py:126
  212.2 4.2 fusion.8
  222.4 202.9 %while.57 = (s32[]{:T(128)}, f32[256,2,4,128]{3,0,2,1:T(8,128)S(1)}, bf16[256,256]{1,0:T(8,128)(2,1)}, bf16[256,256]{1,0:T(8,128)(2,1)}, f32[256,256]{0,1:T(8,12...) while((s32[]{:T(128)}, ...), condition=%wide.region_15.16_spmd.clone, body=%wide.region_11.15_spmd.clone.sunk | while | flops 676593664 | bytes 24142468 | solution.py:226
  231.7 5.6 %conditional.6 = (f32[256,2,4,128]{3,0,2,1:T(8,128)S(1)}, f32[256,256]{0,1:T(8,128)S(1)}, f32[256,256]{0,1:T(8,128)S(1)}) conditional(s32[]{:T(128)} %convert_element_type.204, () %tuple.120, (pred[256,256]{0,1:T(8,128)(4,1)}, bf16[256,256]{1,0:T(8,128)(2,1)}, bf16[256,2,4,128]{0,3,2,1:T(8,128)(2,1)}, f32[2,4,256]{2,1,0:T(4,128)}, ...), branch_computations={%region_13.13_spmd, %region_14.14_spmd} | conditional | flops 675282944 | bytes 16203828 | solution.py:179
  240.0 5.5 collective-permute-done.3
  255.6 5.6 %conditional.6 = (f32[256,2,4,128]{3,0,2,1:T(8,128)S(1)}, f32[256,256]{0,1:T(8,128)S(1)}, f32[256,256]{0,1:T(8,128)S(1)}) conditional(s32[]{:T(128)} %convert_element_type.204, () %tuple.120, (pred[256,256]{0,1:T(8,128)(4,1)}, bf16[256,256]{1,0:T(8,128)(2,1)}, bf16[256,2,4,128]{0,3,2,1:T(8,128)(2,1)}, f32[2,4,256]{2,1,0:T(4,128)}, ...), branch_computations={%region_13.13_spmd, %region_14.14_spmd} | conditional | flops 675282944 | bytes 16203828 | solution.py:179
  265.4 3.6 collective-permute-done.3
  279.9 5.6 %conditional.6 = (f32[256,2,4,128]{3,0,2,1:T(8,128)S(1)}, f32[256,256]{0,1:T(8,128)S(1)}, f32[256,256]{0,1:T(8,128)S(1)}) conditional(s32[]{:T(128)} %convert_element_type.204, () %tuple.120, (pred[256,256]{0,1:T(8,128)(4,1)}, bf16[256,256]{1,0:T(8,128)(2,1)}, bf16[256,2,4,128]{0,3,2,1:T(8,128)(2,1)}, f32[2,4,256]{2,1,0:T(4,128)}, ...), branch_computations={%region_13.13_spmd, %region_14.14_spmd} | conditional | flops 675282944 | bytes 16203828 | solution.py:179
  289.7 3.6 collective-permute-done.3
  304.1 5.6 %conditional.6 = (f32[256,2,4,128]{3,0,2,1:T(8,128)S(1)}, f32[256,256]{0,1:T(8,128)S(1)}, f32[256,256]{0,1:T(8,128)S(1)}) conditional(s32[]{:T(128)} %convert_element_type.204, () %tuple.120, (pred[256,256]{0,1:T(8,128)(4,1)}, bf16[256,256]{1,0:T(8,128)(2,1)}, bf16[256,2,4,128]{0,3,2,1:T(8,128)(2,1)}, f32[2,4,256]{2,1,0:T(4,128)}, ...), branch_computations={%region_13.13_spmd, %region_14.14_spmd} | conditional | flops 675282944 | bytes 16203828 | solution.py:179
  314.4 3.0 collective-permute-done.3
  317.4 3.7 collective-permute-done.2
  331.5 5.6 %conditional.6 = (f32[256,2,4,128]{3,0,2,1:T(8,128)S(1)}, f32[256,256]{0,1:T(8,128)S(1)}, f32[256,256]{0,1:T(8,128)S(1)}) conditional(s32[]{:T(128)} %convert_element_type.204, () %tuple.120, (pred[256,256]{0,1:T(8,128)(4,1)}, bf16[256,256]{1,0:T(8,128)(2,1)}, bf16[256,2,4,128]{0,3,2,1:T(8,128)(2,1)}, f32[2,4,256]{2,1,0:T(4,128)}, ...), branch_computations={%region_13.13_spmd, %region_14.14_spmd} | conditional | flops 675282944 | bytes 16203828 | solution.py:179
  339.2 7.0 %collective-permute-done.3 = bf16[256,256]{0,1:T(8,128)(2,1)S(1)} collective-permute-done((bf16[256,256]{0,1:T(8,128)(2,1)S(1)}, bf16[256,256]{0,1:T(8,128)(2,1)S(1)}, u32[]{:S(2)}, u32[]{:S(2)}) %collective-permute-start.3) | collective-permute-done | bytes 131104 | tf_op jit(solution)/shard_map/while/body/eval_jaxpr/ppermute | solution.py:15
  357.0 5.6 %conditional.6 = (f32[256,2,4,128]{3,0,2,1:T(8,128)S(1)}, f32[256,256]{0,1:T(8,128)S(1)}, f32[256,256]{0,1:T(8,128)S(1)}) conditional(s32[]{:T(128)} %convert_element_type.204, () %tuple.120, (pred[256,256]{0,1:T(8,128)(4,1)}, bf16[256,256]{1,0:T(8,128)(2,1)}, bf16[256,2,4,128]{0,3,2,1:T(8,128)(2,1)}, f32[2,4,256]{2,1,0:T(4,128)}, ...), branch_computations={%region_13.13_spmd, %region_14.14_spmd} | conditional | flops 675282944 | bytes 16203828 | solution.py:179
  366.7 4.1 collective-permute-done.3
  381.7 5.6 %conditional.6 = (f32[256,2,4,128]{3,0,2,1:T(8,128)S(1)}, f32[256,256]{0,1:T(8,128)S(1)}, f32[256,256]{0,1:T(8,128)S(1)}) conditional(s32[]{:T(128)} %convert_element_type.204, () %tuple.120, (pred[256,256]{0,1:T(8,128)(4,1)}, bf16[256,256]{1,0:T(8,128)(2,1)}, bf16[256,2,4,128]{0,3,2,1:T(8,128)(2,1)}, f32[2,4,256]{2,1,0:T(4,128)}, ...), branch_computations={%region_13.13_spmd, %region_14.14_spmd} | conditional | flops 675282944 | bytes 16203828 | solution.py:179
  389.0 2.9 collective-permute-start.2
  392.2 4.1 collective-permute-done.3
  408.2 5.6 %conditional.6 = (f32[256,2,4,128]{3,0,2,1:T(8,128)S(1)}, f32[256,256]{0,1:T(8,128)S(1)}, f32[256,256]{0,1:T(8,128)S(1)}) conditional(s32[]{:T(128)} %convert_element_type.204, () %tuple.120, (pred[256,256]{0,1:T(8,128)(4,1)}, bf16[256,256]{1,0:T(8,128)(2,1)}, bf16[256,2,4,128]{0,3,2,1:T(8,128)(2,1)}, f32[2,4,256]{2,1,0:T(4,128)}, ...), branch_computations={%region_13.13_spmd, %region_14.14_spmd} | conditional | flops 675282944 | bytes 16203828 | solution.py:179
  416.9 6.0 %collective-permute-done.3 = bf16[256,256]{0,1:T(8,128)(2,1)S(1)} collective-permute-done((bf16[256,256]{0,1:T(8,128)(2,1)S(1)}, bf16[256,256]{0,1:T(8,128)(2,1)S(1)}, u32[]{:S(2)}, u32[]{:S(2)}) %collective-permute-start.3) | collective-permute-done | bytes 131104 | tf_op jit(solution)/shard_map/while/body/eval_jaxpr/ppermute | solution.py:15
  426.5 3.4 all-to-all-start.5
  432.1 6.0 %all-to-all-done.5 = bf16[8,64,256]{2,1,0:T(8,128)(2,1)S(1)} async-done(((bf16[8,64,256]{2,1,0:T(8,128)(2,1)}), bf16[8,64,256]{2,1,0:T(8,128)(2,1)S(1)}, u32[]{:S(2)}, u32[]{:S(2)}) %all-to-all-start.5) | async-done | bytes 262176 | tf_op jit(solution)/shard_map/all_to_all | solution.py:240
  438.1 3.6 all-to-all-start.4
  444.8 9.6 %all-to-all-done.4 = bf16[8,64,256]{2,1,0:T(8,128)(2,1)S(1)} async-done(((bf16[8,64,256]{2,1,0:T(8,128)(2,1)}), bf16[8,64,256]{2,1,0:T(8,128)(2,1)S(1)}, u32[]{:S(2)}, u32[]{:S(2)}) %all-to-all-start.4) | async-done | bytes 262176 | tf_op jit(solution)/shard_map/all_to_all | solution.py:237
  454.5 3.6 all-to-all-start.3
  458.7 15.6 %all-to-all-done.3 = bf16[8,64,1024]{2,1,0:T(8,128)(2,1)S(1)} async-done(((bf16[8,64,1024]{2,1,0:T(8,128)(2,1)}), bf16[8,64,1024]{2,1,0:T(8,128)(2,1)S(1)}, u32[]{:S(2)}, u32[]{:S(2)}) %all-to-all-start.3) | async-done | bytes 1048608 | tf_op jit(solution)/shard_map/all_to_all | solution.py:234
  475.3 18.9 %fusion.56 = f32[256,8192]{1,0:T(8,128)} fusion(bf16[256,1024]{1,0:T(8,128)(2,1)S(1)} %bitcast.128, bf16[8192,1024]{1,0:T(8,128)(2,1)} %param.16), kind=kOutput, calls=%fused_computation.91 | convolution fusion | flops 4294967296 | bytes 25690112 | tf_op jit(solution)/shard_map/dot_general | solution.py:43
  494.2 6.1 %convolution_add_fusion.1 = f32[256,8192]{1,0:T(8,128)S(1)} fusion(f32[256,8192]{1,0:T(8,128)} %fusion.56, bf16[256,256]{1,0:T(8,128)(2,1)S(1)} %bitcast.133, bf16[8192,256]{1,0:T(8,128)(2,1)} %param.17), kind=kOutput, calls=%fused_computation.39 | convolution fusion | flops 1075838976 | bytes 21102592 | tf_op jit(solution)/shard_map/dot_general | solution.py:43
  500.3 3.3 fusion.24
  506.2 40.6 %reduce-scatter.2.cloned.1.call-done = bf16[256,2048]{1,0:T(8,128)(2,1)} async-done(((bf16[256,8192]{1,0:T(8,128)(2,1)}), bf16[256,2048]{1,0:T(8,128)(2,1)}) %reduce-scatter.2.cloned.1.call-update) | async-done | bytes 1048592 | tf_op jit(solution)/shard_map/reduce_scatter | solution.py:259
  (343 shorter events, 219.1 us)
Async XLA Ops:
  7.2 39.6 %all-gather.4.cloned.1.call-start = ((), (), s32[]{:S(2)}) async-start(), calls=%async_computation.7 | async-start | bytes 5242880 | tf_op jit(solution)/shard_map/all_gather | solution.py:62
  8.6 75.0 %copy-start.6 = (s32[4]{0:T(128)}, s32[4]{0:T(128)S(1)}, u32[]{:S(2)}) copy-start(s32[4]{0:T(128)S(1)} %dynamic_slice.75) | copy-start | bytes 52
  9.7 115.9 %copy-start.8 = (s32[4]{0:T(128)}, s32[4]{0:T(128)S(1)}, u32[]{:S(2)}) copy-start(s32[4]{0:T(128)S(1)} %and_select_fusion) | copy-start | bytes 52
  52.6 14.8 %all-to-all-start.2 = ((bf16[8,64,256]{2,1,0:T(8,128)(2,1)}), bf16[8,64,256]{2,1,0:T(8,128)(2,1)S(1)}, u32[]{:S(2)}, u32[]{:S(2)}) async-start(bf16[8,64,256]{2,1,0:T(8,128)(2,1)} %copy.111), calls=%async_computation.2 | async-start | bytes 524288 | tf_op jit(solution)/shard_map/all_to_all | solution.py:83
  67.4 18.4 %all-to-all-start = ((bf16[8,64,256]{2,1,0:T(8,128)(2,1)}), bf16[8,64,256]{2,1,0:T(8,128)(2,1)S(1)}, u32[]{:S(2)}, u32[]{:S(2)}) async-start(bf16[8,64,256]{2,1,0:T(8,128)(2,1)} %copy.103), calls=%async_computation | async-start | bytes 524288 | tf_op jit(solution)/shard_map/all_to_all | solution.py:80
  71.0 57.1 %all-gather.8.cloned.1.call-start = ((), (), s32[]{:S(2)}) async-start(), calls=%async_computation.9 | async-start | bytes 1179648 | tf_op jit(solution)/shard_map/all_gather | solution.py:189
  83.6 9.2 %copy-start.10 = (s32[8]{0:T(128)S(1)}, s32[8]{0:T(128)}, u32[]{:S(2)}) copy-start(s32[8]{0:T(128)} %param.19) | copy-start | bytes 100
  83.6 14.2 %copy-start.5 = (bf16[256,1024]{1,0:T(8,128)(2,1)S(1)}, bf16[256,1024]{1,0:T(8,128)(2,1)}, u32[]{:S(2)}) copy-start(bf16[256,1024]{1,0:T(8,128)(2,1)} %param.21) | copy-start | bytes 1572868
  85.8 39.7 %all-to-all-start.1 = ((bf16[8,64,1024]{2,1,0:T(8,128)(2,1)}), bf16[8,64,1024]{2,1,0:T(8,128)(2,1)S(1)}, u32[]{:S(2)}, u32[]{:S(2)}) async-start(bf16[8,64,1024]{2,1,0:T(8,128)(2,1)} %copy.107), calls=%async_computation.1 | async-start | bytes 2097152 | tf_op jit(solution)/shard_map/all_to_all | solution.py:77
  91.8 74.8 %all-gather.6.cloned.1.call-start = ((), (), s32[]{:S(2)}) async-start(), calls=%async_computation.8 | async-start | bytes 1179648 | tf_op jit(solution)/shard_map/all_gather | solution.py:188
  222.4 203.0 %copy-start.9 = (s32[4]{0:T(128)S(1)}, s32[4]{0:T(128)}, u32[]{:S(2)}) copy-start(s32[4]{0:T(128)} %copy-done.8) | copy-start | bytes 52
  224.0 23.6 %collective-permute-start = (bf16[256,256]{1,0:T(8,128)(2,1)}, bf16[256,256]{1,0:T(8,128)(2,1)}, u32[]{:S(2)}, u32[]{:S(2)}) collective-permute-start(bf16[256,256]{1,0:T(8,128)(2,1)} %copy.227), channel_id=1, source_target_pairs={{0,4},{4,8},{8,12},{12,16},{16,20},{20,24},{24,28},{28,0},{1,5},{5... | collective-permute-start | bytes 393224 | tf_op jit(solution)/shard_map/while/body/eval_jaxpr/ppermute | solution.py:15
  226.1 21.5 %collective-permute-start.1 = (bf16[256,256]{1,0:T(8,128)(2,1)}, bf16[256,256]{1,0:T(8,128)(2,1)}, u32[]{:S(2)}, u32[]{:S(2)}) collective-permute-start(bf16[256,256]{1,0:T(8,128)(2,1)} %copy.228), channel_id=1, source_target_pairs={{0,4},{4,8},{8,12},{12,16},{16,20},{20,24},{24,28},{28,0},{1,5},{5... | collective-permute-start | bytes 393224 | tf_op jit(solution)/shard_map/while/body/eval_jaxpr/ppermute | solution.py:15
  237.3 8.2 %collective-permute-start.3 = (bf16[256,256]{0,1:T(8,128)(2,1)S(1)}, bf16[256,256]{0,1:T(8,128)(2,1)S(1)}, u32[]{:S(2)}, u32[]{:S(2)}) collective-permute-start(bf16[256,256]{0,1:T(8,128)(2,1)S(1)} %fusion.85), channel_id=1, source_target_pairs={{0,4},{4,8},{8,12},{12,16},{16,20},{20,24},{24,28},{28,0},{1,5},{5... | collective-permute-start | bytes 393224 | tf_op jit(solution)/shard_map/while/body/eval_jaxpr/ppermute | solution.py:15
  238.0 8.9 %collective-permute-start.2 = (bf16[256,256]{0,1:T(8,128)(2,1)S(1)}, bf16[256,256]{0,1:T(8,128)(2,1)S(1)}, u32[]{:S(2)}, u32[]{:S(2)}) collective-permute-start(bf16[256,256]{0,1:T(8,128)(2,1)S(1)} %fusion.84), channel_id=1, source_target_pairs={{0,4},{4,8},{8,12},{12,16},{16,20},{20,24},{24,28},{28,0},{1,5},{5... | collective-permute-start | bytes 393224 | tf_op jit(solution)/shard_map/while/body/eval_jaxpr/ppermute | solution.py:15
  249.2 22.0 %collective-permute-start = (bf16[256,256]{1,0:T(8,128)(2,1)}, bf16[256,256]{1,0:T(8,128)(2,1)}, u32[]{:S(2)}, u32[]{:S(2)}) collective-permute-start(bf16[256,256]{1,0:T(8,128)(2,1)} %copy.227), channel_id=1, source_target_pairs={{0,4},{4,8},{8,12},{12,16},{16,20},{20,24},{24,28},{28,0},{1,5},{5... | collective-permute-start | bytes 393224 | tf_op jit(solution)/shard_map/while/body/eval_jaxpr/ppermute | solution.py:15
  250.8 20.4 %collective-permute-start.1 = (bf16[256,256]{1,0:T(8,128)(2,1)}, bf16[256,256]{1,0:T(8,128)(2,1)}, u32[]{:S(2)}, u32[]{:S(2)}) collective-permute-start(bf16[256,256]{1,0:T(8,128)(2,1)} %copy.228), channel_id=1, source_target_pairs={{0,4},{4,8},{8,12},{12,16},{16,20},{20,24},{24,28},{28,0},{1,5},{5... | collective-permute-start | bytes 393224 | tf_op jit(solution)/shard_map/while/body/eval_jaxpr/ppermute | solution.py:15
  261.2 7.7 %collective-permute-start.3 = (bf16[256,256]{0,1:T(8,128)(2,1)S(1)}, bf16[256,256]{0,1:T(8,128)(2,1)S(1)}, u32[]{:S(2)}, u32[]{:S(2)}) collective-permute-start(bf16[256,256]{0,1:T(8,128)(2,1)S(1)} %fusion.85), channel_id=1, source_target_pairs={{0,4},{4,8},{8,12},{12,16},{16,20},{20,24},{24,28},{28,0},{1,5},{5... | collective-permute-start | bytes 393224 | tf_op jit(solution)/shard_map/while/body/eval_jaxpr/ppermute | solution.py:15
  262.8 7.7 %collective-permute-start.2 = (bf16[256,256]{0,1:T(8,128)(2,1)S(1)}, bf16[256,256]{0,1:T(8,128)(2,1)S(1)}, u32[]{:S(2)}, u32[]{:S(2)}) collective-permute-start(bf16[256,256]{0,1:T(8,128)(2,1)S(1)} %fusion.84), channel_id=1, source_target_pairs={{0,4},{4,8},{8,12},{12,16},{16,20},{20,24},{24,28},{28,0},{1,5},{5... | collective-permute-start | bytes 393224 | tf_op jit(solution)/shard_map/while/body/eval_jaxpr/ppermute | solution.py:15
  272.8 23.7 %collective-permute-start = (bf16[256,256]{1,0:T(8,128)(2,1)}, bf16[256,256]{1,0:T(8,128)(2,1)}, u32[]{:S(2)}, u32[]{:S(2)}) collective-permute-start(bf16[256,256]{1,0:T(8,128)(2,1)} %copy.227), channel_id=1, source_target_pairs={{0,4},{4,8},{8,12},{12,16},{16,20},{20,24},{24,28},{28,0},{1,5},{5... | collective-permute-start | bytes 393224 | tf_op jit(solution)/shard_map/while/body/eval_jaxpr/ppermute | solution.py:15
  274.4 22.1 %collective-permute-start.1 = (bf16[256,256]{1,0:T(8,128)(2,1)}, bf16[256,256]{1,0:T(8,128)(2,1)}, u32[]{:S(2)}, u32[]{:S(2)}) collective-permute-start(bf16[256,256]{1,0:T(8,128)(2,1)} %copy.228), channel_id=1, source_target_pairs={{0,4},{4,8},{8,12},{12,16},{16,20},{20,24},{24,28},{28,0},{1,5},{5... | collective-permute-start | bytes 393224 | tf_op jit(solution)/shard_map/while/body/eval_jaxpr/ppermute | solution.py:15
  285.5 7.7 %collective-permute-start.3 = (bf16[256,256]{0,1:T(8,128)(2,1)S(1)}, bf16[256,256]{0,1:T(8,128)(2,1)S(1)}, u32[]{:S(2)}, u32[]{:S(2)}) collective-permute-start(bf16[256,256]{0,1:T(8,128)(2,1)S(1)} %fusion.85), channel_id=1, source_target_pairs={{0,4},{4,8},{8,12},{12,16},{16,20},{20,24},{24,28},{28,0},{1,5},{5... | collective-permute-start | bytes 393224 | tf_op jit(solution)/shard_map/while/body/eval_jaxpr/ppermute | solution.py:15
  288.0 7.7 %collective-permute-start.2 = (bf16[256,256]{0,1:T(8,128)(2,1)S(1)}, bf16[256,256]{0,1:T(8,128)(2,1)S(1)}, u32[]{:S(2)}, u32[]{:S(2)}) collective-permute-start(bf16[256,256]{0,1:T(8,128)(2,1)S(1)} %fusion.84), channel_id=1, source_target_pairs={{0,4},{4,8},{8,12},{12,16},{16,20},{20,24},{24,28},{28,0},{1,5},{5... | collective-permute-start | bytes 393224 | tf_op jit(solution)/shard_map/while/body/eval_jaxpr/ppermute | solution.py:15
  298.1 23.9 %collective-permute-start = (bf16[256,256]{1,0:T(8,128)(2,1)}, bf16[256,256]{1,0:T(8,128)(2,1)}, u32[]{:S(2)}, u32[]{:S(2)}) collective-permute-start(bf16[256,256]{1,0:T(8,128)(2,1)} %copy.227), channel_id=1, source_target_pairs={{0,4},{4,8},{8,12},{12,16},{16,20},{20,24},{24,28},{28,0},{1,5},{5... | collective-permute-start | bytes 393224 | tf_op jit(solution)/shard_map/while/body/eval_jaxpr/ppermute | solution.py:15
  299.6 22.3 %collective-permute-start.1 = (bf16[256,256]{1,0:T(8,128)(2,1)}, bf16[256,256]{1,0:T(8,128)(2,1)}, u32[]{:S(2)}, u32[]{:S(2)}) collective-permute-start(bf16[256,256]{1,0:T(8,128)(2,1)} %copy.228), channel_id=1, source_target_pairs={{0,4},{4,8},{8,12},{12,16},{16,20},{20,24},{24,28},{28,0},{1,5},{5... | collective-permute-start | bytes 393224 | tf_op jit(solution)/shard_map/while/body/eval_jaxpr/ppermute | solution.py:15
  309.7 7.7 %collective-permute-start.3 = (bf16[256,256]{0,1:T(8,128)(2,1)S(1)}, bf16[256,256]{0,1:T(8,128)(2,1)S(1)}, u32[]{:S(2)}, u32[]{:S(2)}) collective-permute-start(bf16[256,256]{0,1:T(8,128)(2,1)S(1)} %fusion.85), channel_id=1, source_target_pairs={{0,4},{4,8},{8,12},{12,16},{16,20},{20,24},{24,28},{28,0},{1,5},{5... | collective-permute-start | bytes 393224 | tf_op jit(solution)/shard_map/while/body/eval_jaxpr/ppermute | solution.py:15
  313.2 8.0 %collective-permute-start.2 = (bf16[256,256]{0,1:T(8,128)(2,1)S(1)}, bf16[256,256]{0,1:T(8,128)(2,1)S(1)}, u32[]{:S(2)}, u32[]{:S(2)}) collective-permute-start(bf16[256,256]{0,1:T(8,128)(2,1)S(1)} %fusion.84), channel_id=1, source_target_pairs={{0,4},{4,8},{8,12},{12,16},{16,20},{20,24},{24,28},{28,0},{1,5},{5... | collective-permute-start | bytes 393224 | tf_op jit(solution)/shard_map/while/body/eval_jaxpr/ppermute | solution.py:15
  323.5 26.3 %collective-permute-start = (bf16[256,256]{1,0:T(8,128)(2,1)}, bf16[256,256]{1,0:T(8,128)(2,1)}, u32[]{:S(2)}, u32[]{:S(2)}) collective-permute-start(bf16[256,256]{1,0:T(8,128)(2,1)} %copy.227), channel_id=1, source_target_pairs={{0,4},{4,8},{8,12},{12,16},{16,20},{20,24},{24,28},{28,0},{1,5},{5... | collective-permute-start | bytes 393224 | tf_op jit(solution)/shard_map/while/body/eval_jaxpr/ppermute | solution.py:15
  325.1 24.7 %collective-permute-start.1 = (bf16[256,256]{1,0:T(8,128)(2,1)}, bf16[256,256]{1,0:T(8,128)(2,1)}, u32[]{:S(2)}, u32[]{:S(2)}) collective-permute-start(bf16[256,256]{1,0:T(8,128)(2,1)} %copy.228), channel_id=1, source_target_pairs={{0,4},{4,8},{8,12},{12,16},{16,20},{20,24},{24,28},{28,0},{1,5},{5... | collective-permute-start | bytes 393224 | tf_op jit(solution)/shard_map/while/body/eval_jaxpr/ppermute | solution.py:15
  337.2 9.1 %collective-permute-start.3 = (bf16[256,256]{0,1:T(8,128)(2,1)S(1)}, bf16[256,256]{0,1:T(8,128)(2,1)S(1)}, u32[]{:S(2)}, u32[]{:S(2)}) collective-permute-start(bf16[256,256]{0,1:T(8,128)(2,1)S(1)} %fusion.85), channel_id=1, source_target_pairs={{0,4},{4,8},{8,12},{12,16},{16,20},{20,24},{24,28},{28,0},{1,5},{5... | collective-permute-start | bytes 393224 | tf_op jit(solution)/shard_map/while/body/eval_jaxpr/ppermute | solution.py:15
  338.8 10.2 %collective-permute-start.2 = (bf16[256,256]{0,1:T(8,128)(2,1)S(1)}, bf16[256,256]{0,1:T(8,128)(2,1)S(1)}, u32[]{:S(2)}, u32[]{:S(2)}) collective-permute-start(bf16[256,256]{0,1:T(8,128)(2,1)S(1)} %fusion.84), channel_id=1, source_target_pairs={{0,4},{4,8},{8,12},{12,16},{16,20},{20,24},{24,28},{28,0},{1,5},{5... | collective-permute-start | bytes 393224 | tf_op jit(solution)/shard_map/while/body/eval_jaxpr/ppermute | solution.py:15
  351.3 21.6 %collective-permute-start = (bf16[256,256]{1,0:T(8,128)(2,1)}, bf16[256,256]{1,0:T(8,128)(2,1)}, u32[]{:S(2)}, u32[]{:S(2)}) collective-permute-start(bf16[256,256]{1,0:T(8,128)(2,1)} %copy.227), channel_id=1, source_target_pairs={{0,4},{4,8},{8,12},{12,16},{16,20},{20,24},{24,28},{28,0},{1,5},{5... | collective-permute-start | bytes 393224 | tf_op jit(solution)/shard_map/while/body/eval_jaxpr/ppermute | solution.py:15
  352.9 20.1 %collective-permute-start.1 = (bf16[256,256]{1,0:T(8,128)(2,1)}, bf16[256,256]{1,0:T(8,128)(2,1)}, u32[]{:S(2)}, u32[]{:S(2)}) collective-permute-start(bf16[256,256]{1,0:T(8,128)(2,1)} %copy.228), channel_id=1, source_target_pairs={{0,4},{4,8},{8,12},{12,16},{16,20},{20,24},{24,28},{28,0},{1,5},{5... | collective-permute-start | bytes 393224 | tf_op jit(solution)/shard_map/while/body/eval_jaxpr/ppermute | solution.py:15
  362.7 8.1 %collective-permute-start.3 = (bf16[256,256]{0,1:T(8,128)(2,1)S(1)}, bf16[256,256]{0,1:T(8,128)(2,1)S(1)}, u32[]{:S(2)}, u32[]{:S(2)}) collective-permute-start(bf16[256,256]{0,1:T(8,128)(2,1)S(1)} %fusion.85), channel_id=1, source_target_pairs={{0,4},{4,8},{8,12},{12,16},{16,20},{20,24},{24,28},{28,0},{1,5},{5... | collective-permute-start | bytes 393224 | tf_op jit(solution)/shard_map/while/body/eval_jaxpr/ppermute | solution.py:15
  363.7 8.5 %collective-permute-start.2 = (bf16[256,256]{0,1:T(8,128)(2,1)S(1)}, bf16[256,256]{0,1:T(8,128)(2,1)S(1)}, u32[]{:S(2)}, u32[]{:S(2)}) collective-permute-start(bf16[256,256]{0,1:T(8,128)(2,1)S(1)} %fusion.84), channel_id=1, source_target_pairs={{0,4},{4,8},{8,12},{12,16},{16,20},{20,24},{24,28},{28,0},{1,5},{5... | collective-permute-start | bytes 393224 | tf_op jit(solution)/shard_map/while/body/eval_jaxpr/ppermute | solution.py:15
  374.5 24.0 %collective-permute-start = (bf16[256,256]{1,0:T(8,128)(2,1)}, bf16[256,256]{1,0:T(8,128)(2,1)}, u32[]{:S(2)}, u32[]{:S(2)}) collective-permute-start(bf16[256,256]{1,0:T(8,128)(2,1)} %copy.227), channel_id=1, source_target_pairs={{0,4},{4,8},{8,12},{12,16},{16,20},{20,24},{24,28},{28,0},{1,5},{5... | collective-permute-start | bytes 393224 | tf_op jit(solution)/shard_map/while/body/eval_jaxpr/ppermute | solution.py:15
  376.1 22.5 %collective-permute-start.1 = (bf16[256,256]{1,0:T(8,128)(2,1)}, bf16[256,256]{1,0:T(8,128)(2,1)}, u32[]{:S(2)}, u32[]{:S(2)}) collective-permute-start(bf16[256,256]{1,0:T(8,128)(2,1)} %copy.228), channel_id=1, source_target_pairs={{0,4},{4,8},{8,12},{12,16},{16,20},{20,24},{24,28},{28,0},{1,5},{5... | collective-permute-start | bytes 393224 | tf_op jit(solution)/shard_map/while/body/eval_jaxpr/ppermute | solution.py:15
  387.3 9.0 %collective-permute-start.3 = (bf16[256,256]{0,1:T(8,128)(2,1)S(1)}, bf16[256,256]{0,1:T(8,128)(2,1)S(1)}, u32[]{:S(2)}, u32[]{:S(2)}) collective-permute-start(bf16[256,256]{0,1:T(8,128)(2,1)S(1)} %fusion.85), channel_id=1, source_target_pairs={{0,4},{4,8},{8,12},{12,16},{16,20},{20,24},{24,28},{28,0},{1,5},{5... | collective-permute-start | bytes 393224 | tf_op jit(solution)/shard_map/while/body/eval_jaxpr/ppermute | solution.py:15
  389.0 8.8 %collective-permute-start.2 = (bf16[256,256]{0,1:T(8,128)(2,1)S(1)}, bf16[256,256]{0,1:T(8,128)(2,1)S(1)}, u32[]{:S(2)}, u32[]{:S(2)}) collective-permute-start(bf16[256,256]{0,1:T(8,128)(2,1)S(1)} %fusion.84), channel_id=1, source_target_pairs={{0,4},{4,8},{8,12},{12,16},{16,20},{20,24},{24,28},{28,0},{1,5},{5... | collective-permute-start | bytes 393224 | tf_op jit(solution)/shard_map/while/body/eval_jaxpr/ppermute | solution.py:15
  400.1 25.2 %collective-permute-start = (bf16[256,256]{1,0:T(8,128)(2,1)}, bf16[256,256]{1,0:T(8,128)(2,1)}, u32[]{:S(2)}, u32[]{:S(2)}) collective-permute-start(bf16[256,256]{1,0:T(8,128)(2,1)} %copy.227), channel_id=1, source_target_pairs={{0,4},{4,8},{8,12},{12,16},{16,20},{20,24},{24,28},{28,0},{1,5},{5... | collective-permute-start | bytes 393224 | tf_op jit(solution)/shard_map/while/body/eval_jaxpr/ppermute | solution.py:15
  401.7 23.6 %collective-permute-start.1 = (bf16[256,256]{1,0:T(8,128)(2,1)}, bf16[256,256]{1,0:T(8,128)(2,1)}, u32[]{:S(2)}, u32[]{:S(2)}) collective-permute-start(bf16[256,256]{1,0:T(8,128)(2,1)} %copy.228), channel_id=1, source_target_pairs={{0,4},{4,8},{8,12},{12,16},{16,20},{20,24},{24,28},{28,0},{1,5},{5... | collective-permute-start | bytes 393224 | tf_op jit(solution)/shard_map/while/body/eval_jaxpr/ppermute | solution.py:15
  413.8 9.0 %collective-permute-start.3 = (bf16[256,256]{0,1:T(8,128)(2,1)S(1)}, bf16[256,256]{0,1:T(8,128)(2,1)S(1)}, u32[]{:S(2)}, u32[]{:S(2)}) collective-permute-start(bf16[256,256]{0,1:T(8,128)(2,1)S(1)} %fusion.85), channel_id=1, source_target_pairs={{0,4},{4,8},{8,12},{12,16},{16,20},{20,24},{24,28},{28,0},{1,5},{5... | collective-permute-start | bytes 393224 | tf_op jit(solution)/shard_map/while/body/eval_jaxpr/ppermute | solution.py:15
  415.2 9.4 %collective-permute-start.2 = (bf16[256,256]{0,1:T(8,128)(2,1)S(1)}, bf16[256,256]{0,1:T(8,128)(2,1)S(1)}, u32[]{:S(2)}, u32[]{:S(2)}) collective-permute-start(bf16[256,256]{0,1:T(8,128)(2,1)S(1)} %fusion.84), channel_id=1, source_target_pairs={{0,4},{4,8},{8,12},{12,16},{16,20},{20,24},{24,28},{28,0},{1,5},{5... | collective-permute-start | bytes 393224 | tf_op jit(solution)/shard_map/while/body/eval_jaxpr/ppermute | solution.py:15
  426.5 11.6 %all-to-all-start.5 = ((bf16[8,64,256]{2,1,0:T(8,128)(2,1)}), bf16[8,64,256]{2,1,0:T(8,128)(2,1)S(1)}, u32[]{:S(2)}, u32[]{:S(2)}) async-start(bf16[8,64,256]{2,1,0:T(8,128)(2,1)} %copy.132), calls=%async_computation.5 | async-start | bytes 524288 | tf_op jit(solution)/shard_map/all_to_all | solution.py:240
  438.1 16.4 %all-to-all-start.4 = ((bf16[8,64,256]{2,1,0:T(8,128)(2,1)}), bf16[8,64,256]{2,1,0:T(8,128)(2,1)S(1)}, u32[]{:S(2)}, u32[]{:S(2)}) async-start(bf16[8,64,256]{2,1,0:T(8,128)(2,1)} %copy.127), calls=%async_computation.4 | async-start | bytes 524288 | tf_op jit(solution)/shard_map/all_to_all | solution.py:237
  441.8 16.3 %copy-start.7 = (s32[4]{0:T(128)S(1)}, s32[4]{0:T(128)}, u32[]{:S(2)}) copy-start(s32[4]{0:T(128)} %copy-done.6) | copy-start | bytes 52
  454.5 19.9 %all-to-all-start.3 = ((bf16[8,64,1024]{2,1,0:T(8,128)(2,1)}), bf16[8,64,1024]{2,1,0:T(8,128)(2,1)S(1)}, u32[]{:S(2)}, u32[]{:S(2)}) async-start(bf16[8,64,1024]{2,1,0:T(8,128)(2,1)} %copy.122), calls=%async_computation.3 | async-start | bytes 2097152 | tf_op jit(solution)/shard_map/all_to_all | solution.py:234
  458.0 88.7 %reduce-scatter.2.cloned.1.call-start = ((), (), s32[]{:S(2)}) async-start(), calls=%async_computation.10 | async-start | bytes 5242880 | tf_op jit(solution)/shard_map/reduce_scatter | solution.py:259
  (18 other events, 40.0 us)
Sparse Core Ops, SparseCore 0:
  9.6 37.1 all-gather.3
  74.0 51.0 all-gather.7
  127.2 39.3 all-gather.5
  503.7 43.0 reduce-scatter.1
where the time goes:
time: 556 us; the launch traced here: 553 us
  waiting for transfers between devices  231 us (42%)
  matrix products  104 us (19%)
  local copies, waits for them, and re-layouts  90.9 us (16%)
  starting transfers between devices  56.4 us (10%)
  other arithmetic  49 us (9%)
  between operations  14.1 us (3%)
  loops' own time  8.15 us (1%)
    ppermute x32, waiting for transfers between devices, from_behind(): return lax.ppermute(value, axis, pairs)  53.3 us
    reduce_scatter x1, waiting for transfers between devices, per_device(): lax.psum_scatter(grad_terms.astype(jnp.bfloat16), 'heads', scatter_dimens...  40.6 us
    all_gather x1, waiting for transfers between devices, per_device(): piece = lax.all_gather(activations, 'heads', axis=1, tiled=True)  37.1 us
    all_gather x1, waiting for transfers between devices, per_device(): key_piece = lax.all_gather(ctx_k, 'ctx', axis=0, tiled=True)  36.9 us
    ppermute x32, starting transfers between devices, from_behind(): return lax.ppermute(value, axis, pairs)  30.5 us
    dot_general x3, matrix products, transposed_dot(): lax.dot_general(left, weight, (((1,), (1,)), ((), ())), preferred_element...  28.3 us
    all_to_all x1, waiting for transfers between devices, per_device(): lax.all_to_all(spread(send_map, loader_q, block_rows), 'ctx', split_axis=...  27.5 us
    while x16, local copies, waits for them, and re-layouts  25 us
  transfers between devices with their start and end apart: 42, of which 24 were waited for; matrix products, arithmetic and copies ran while one was open for 25% of the time, Pallas kernels for 0%

commit v1 on v0

--- a/solution.py
+++ b/solution.py
@@ -185,7 +185,23 @@
         return lax.fori_loop(0, rows // width, grads_one_block, (dquery, empty_rows, empty_rows))
 
     dq_start = jnp.zeros((tok_dev, groups, per_group, head_dim), jnp.float32)
-    key_piece = lax.all_gather(ctx_k, "ctx", axis=0, tiled=True)
+    count_2, place, extent = (lax.axis_size("ctx"), lax.axis_index("ctx"), ctx_k.shape[0])
+    right = [(i, (i + 1) % count_2) for i in range(count_2)]
+    backward = [(i, (i - 1) % count_2) for i in range(count_2)]
+    key_piece = jnp.zeros((*ctx_k.shape[:0], count_2 * extent, *ctx_k.shape[0 + 1 :]), ctx_k.dtype)
+    key_piece = lax.dynamic_update_slice_in_dim(key_piece, ctx_k, place * extent, axis=0)
+    from_left = from_right = ctx_k
+    middle = count_2 // 2
+    for k in range(1, middle + 1):
+        from_left = lax.ppermute(from_left, "ctx", right)
+        key_piece = lax.dynamic_update_slice_in_dim(
+            key_piece, from_left, (place - k) % count_2 * extent, axis=0
+        )
+        if k < count_2 - middle:
+            from_right = lax.ppermute(from_right, "ctx", backward)
+            key_piece = lax.dynamic_update_slice_in_dim(
+                key_piece, from_right, (place + k) % count_2 * extent, axis=0
+            )
     value_piece = lax.all_gather(ctx_v, "ctx", axis=0, tiled=True)
     rows = key_piece.shape[0]
     width = math.gcd(rows, 512)

time: 556 us -> 540 us (0.971)
  waiting for transfers between devices: 231 us -> 191 us
  starting transfers between devices: 56.4 us -> 75.6 us
    all_gather x1 -> x0, waiting for transfers between devices: 36.9 us -> none  [per_device(): key_piece = lax.all_gather(ctx_k, 'ctx', axis=0, tiled=True)]
    ppermute x0 -> x7, waiting for transfers between devices: none -> 29.5 us  [the longest x4 24.5 us: per_device(): from_left = lax.ppermute(from_left, 'ctx', right)]
    all_to_all x1, waiting for transfers between devices: 27.5 us -> 0.01 us  [per_device(): lax.all_to_all(spread(send_map, loader_q, block_rows), 'ctx', split_axis=...]
    ppermute x0 -> x7, starting transfers between devices: none -> 16.1 us  [the longest x3 12.8 us: per_device(): from_right = lax.ppermute(from_right, 'ctx', backward)]
  transfers between devices with their start and end apart: 42 -> 48, of which waited for: 24 -> 28; matrix products, arithmetic and copies ran while one was open for 25% -> 27% of each run, Pallas kernels for 0% -> 0%
where the time goes in v1:
time: 540 us; the launch traced here: 537 us
  waiting for transfers between devices  191 us (35%)
  matrix products  106 us (20%)
  local copies, waits for them, and re-layouts  92.1 us (17%)
  starting transfers between devices  75.6 us (14%)
  other arithmetic  48.8 us (9%)
  between operations  14.3 us (3%)
  loops' own time  8.82 us (2%)
    ppermute x32, waiting for transfers between devices, from_behind(): return lax.ppermute(value, axis, pairs)  50.6 us
    reduce_scatter x1, waiting for transfers between devices, per_device(): lax.psum_scatter(grad_terms.astype(jnp.bfloat16), 'heads', scatter_dimens...  39.7 us
    all_gather x1, waiting for transfers between devices, per_device(): piece = lax.all_gather(activations, 'heads', axis=1, tiled=True)  37.1 us
    ppermute x32, starting transfers between devices, from_behind(): return lax.ppermute(value, axis, pairs)  33.7 us
    dot_general x3, matrix products, transposed_dot(): lax.dot_general(left, weight, (((1,), (1,)), ((), ())), preferred_element...  28.3 us
    while x16, local copies, waits for them, and re-layouts  25 us
    ppermute x4, waiting for transfers between devices, per_device(): from_left = lax.ppermute(from_left, 'ctx', right)  24.5 us
    dot_general x4, matrix products, attend_run(): jnp.einsum('gqts,sge->gqte', probs, value_blk.astype(jnp.float32), precis...  16.8 us
  transfers between devices with their start and end apart: 48, of which 28 were waited for; matrix products, arithmetic and copies ran while one was open for 27% of the time, Pallas kernels for 0%

profile of v1, /device:TPU:0, one launch (start us, length us, event | category | flops | bytes accessed | tf_op | source)
XLA Modules:
  0.0 536.7 jit_solution(3715258630182841776)
XLA Ops:
  9.7 37.1 %all-gather.3.cloned.1.call-done = bf16[256,8192]{1,0:T(8,128)(2,1)} async-done(((bf16[256,2048]{1,0:T(8,128)(2,1)}), bf16[256,8192]{1,0:T(8,128)(2,1)}) %all-gather.3.cloned.1.call-update) | async-done | bytes 4194320 | tf_op jit(solution)/shard_map/all_gather | solution.py:62
  46.8 4.7 convolution_convert_fusion.13
  52.6 5.5 %all-to-all-start.2 = ((bf16[8,64,256]{2,1,0:T(8,128)(2,1)}), bf16[8,64,256]{2,1,0:T(8,128)(2,1)S(1)}, u32[]{:S(2)}, u32[]{:S(2)}) async-start(bf16[8,64,256]{2,1,0:T(8,128)(2,1)} %copy.133), calls=%async_computation.2 | async-start | bytes 524288 | tf_op jit(solution)/shard_map/all_to_all | solution.py:83
  58.1 4.7 convolution_convert_fusion.14
  63.9 3.5 all-to-all-done.2
  67.4 3.6 all-to-all-start
  71.0 11.5 %convolution_convert_fusion.4 = bf16[256,1024]{1,0:T(8,128)(2,1)S(1)} fusion(bf16[256,8192]{1,0:T(8,128)(2,1)} %all-gather.3.cloned.1.call-done, bf16[8192,1024]{1,0:T(8,128)(2,1)} %param.16), kind=kOutput, calls=%fused_computation.45 | convolution fusion | flops 4295229440 | bytes 21495808 | tf_op jit(solution)/shard_map/dot_general | solution.py:64
  84.8 6.0 %all-to-all-start.1 = ((bf16[8,64,1024]{2,1,0:T(8,128)(2,1)}), bf16[8,64,1024]{2,1,0:T(8,128)(2,1)}, u32[]{:S(2)}, u32[]{:S(2)}) async-start(bf16[8,64,1024]{2,1,0:T(8,128)(2,1)} %copy.129), calls=%async_computation.1 | async-start | bytes 2097152 | tf_op jit(solution)/shard_map/all_to_all | solution.py:77
  103.9 15.4 %collective-permute-done.4 = bf16[256,256]{1,0:T(8,128)(2,1)S(1)} collective-permute-done((bf16[256,256]{1,0:T(8,128)(2,1)}, bf16[256,256]{1,0:T(8,128)(2,1)S(1)}, u32[]{:S(2)}, u32[]{:S(2)}) %collective-permute-start.4) | collective-permute-done | bytes 131104 | tf_op jit(solution)/shard_map/ppermute | solution.py:196
  119.6 4.8 collective-permute-start.7
  129.2 5.2 collective-permute-start.9
  140.3 5.1 collective-permute-done.10
  154.3 47.7 %while.56 = (s32[]{:T(128)}, f32[2,4,256]{2,1,0:T(4,128)S(1)}, f32[2,4,256]{2,1,0:T(4,128)S(1)}, f32[2,4,256,128]{3,2,1,0:T(8,128)}, s32[256]{0:T(256)}, /*index...) while((s32[]{:T(128)}, f32[2,4,256]{2,1,0:T(4,128)S(1)}, ...), condition=%wide.region_10.11_spmd, body=%wide.region_4.10_spmd.sunk | while | flops 1892683776 | bytes 25835900 | solution.py:221
  158.1 8.2 %conditional.5 = ((f32[2,4,256]{2,1,0:T(4,128)S(1)}, f32[2,4,256]{2,1,0:T(4,128)S(1)}, f32[2,4,256,128]{3,2,1,0:T(8,128)})) conditional(s32[]{:T(128)} %convert_element_type.201, (f32[2,4,256]{2,1,0:T(4,128)S(1)}, f32[2,4,256]{2,1,0:T(4,128)S(1)}, f32[2,4,256,128]{3,2,1,0:T(8,128)}) %tuple.116, (pred[256,512]{0,1:T(8,128)(4,1)S(1)}, ...), branch_computations={%region_6.6_spmd, %region_7.9_spmd} | conditional | flops 1892159488 | bytes 25690204 | solution.py:126
  161.1 4.2 fusion.8
  170.0 8.2 %conditional.5 = ((f32[2,4,256]{2,1,0:T(4,128)S(1)}, f32[2,4,256]{2,1,0:T(4,128)S(1)}, f32[2,4,256,128]{3,2,1,0:T(8,128)})) conditional(s32[]{:T(128)} %convert_element_type.201, (f32[2,4,256]{2,1,0:T(4,128)S(1)}, f32[2,4,256]{2,1,0:T(4,128)S(1)}, f32[2,4,256,128]{3,2,1,0:T(8,128)}) %tuple.116, (pred[256,512]{0,1:T(8,128)(4,1)S(1)}, ...), branch_computations={%region_6.6_spmd, %region_7.9_spmd} | conditional | flops 1892159488 | bytes 25690204 | solution.py:126
  173.0 4.2 fusion.8
  181.9 8.2 %conditional.5 = ((f32[2,4,256]{2,1,0:T(4,128)S(1)}, f32[2,4,256]{2,1,0:T(4,128)S(1)}, f32[2,4,256,128]{3,2,1,0:T(8,128)})) conditional(s32[]{:T(128)} %convert_element_type.201, (f32[2,4,256]{2,1,0:T(4,128)S(1)}, f32[2,4,256]{2,1,0:T(4,128)S(1)}, f32[2,4,256,128]{3,2,1,0:T(8,128)}) %tuple.116, (pred[256,512]{0,1:T(8,128)(4,1)S(1)}, ...), branch_computations={%region_6.6_spmd, %region_7.9_spmd} | conditional | flops 1892159488 | bytes 25690204 | solution.py:126
  184.9 4.2 fusion.8
  193.8 8.2 %conditional.5 = ((f32[2,4,256]{2,1,0:T(4,128)S(1)}, f32[2,4,256]{2,1,0:T(4,128)S(1)}, f32[2,4,256,128]{3,2,1,0:T(8,128)})) conditional(s32[]{:T(128)} %convert_element_type.201, (f32[2,4,256]{2,1,0:T(4,128)S(1)}, f32[2,4,256]{2,1,0:T(4,128)S(1)}, f32[2,4,256,128]{3,2,1,0:T(8,128)}) %tuple.116, (pred[256,512]{0,1:T(8,128)(4,1)S(1)}, ...), branch_computations={%region_6.6_spmd, %region_7.9_spmd} | conditional | flops 1892159488 | bytes 25690204 | solution.py:126
  196.8 4.2 fusion.8
  207.0 203.4 %while.57 = (s32[]{:T(128)}, f32[256,2,4,128]{3,0,2,1:T(8,128)S(1)}, bf16[256,256]{1,0:T(8,128)(2,1)}, bf16[256,256]{1,0:T(8,128)(2,1)}, f32[256,256]{0,1:T(8,12...) while((s32[]{:T(128)}, ...), condition=%wide.region_15.16_spmd.clone, body=%wide.region_11.15_spmd.clone.sunk | while | flops 676593664 | bytes 24142468 | solution.py:242
  217.3 5.6 %conditional.6 = (f32[256,2,4,128]{3,0,2,1:T(8,128)S(1)}, f32[256,256]{0,1:T(8,128)S(1)}, f32[256,256]{0,1:T(8,128)S(1)}) conditional(s32[]{:T(128)} %convert_element_type.204, () %tuple.120, (pred[256,256]{0,1:T(8,128)(4,1)}, bf16[256,256]{1,0:T(8,128)(2,1)}, bf16[256,2,4,128]{0,3,2,1:T(8,128)(2,1)}, f32[2,4,256]{2,1,0:T(4,128)}, ...), branch_computations={%region_13.13_spmd, %region_14.14_spmd} | conditional | flops 675282944 | bytes 16203828 | solution.py:179
  225.7 4.9 collective-permute-done.3
  240.6 5.6 %conditional.6 = (f32[256,2,4,128]{3,0,2,1:T(8,128)S(1)}, f32[256,256]{0,1:T(8,128)S(1)}, f32[256,256]{0,1:T(8,128)S(1)}) conditional(s32[]{:T(128)} %convert_element_type.204, () %tuple.120, (pred[256,256]{0,1:T(8,128)(4,1)}, bf16[256,256]{1,0:T(8,128)(2,1)}, bf16[256,2,4,128]{0,3,2,1:T(8,128)(2,1)}, f32[2,4,256]{2,1,0:T(4,128)}, ...), branch_computations={%region_13.13_spmd, %region_14.14_spmd} | conditional | flops 675282944 | bytes 16203828 | solution.py:179
  250.0 3.9 collective-permute-done.3
  264.6 5.6 %conditional.6 = (f32[256,2,4,128]{3,0,2,1:T(8,128)S(1)}, f32[256,256]{0,1:T(8,128)S(1)}, f32[256,256]{0,1:T(8,128)S(1)}) conditional(s32[]{:T(128)} %convert_element_type.204, () %tuple.120, (pred[256,256]{0,1:T(8,128)(4,1)}, bf16[256,256]{1,0:T(8,128)(2,1)}, bf16[256,2,4,128]{0,3,2,1:T(8,128)(2,1)}, f32[2,4,256]{2,1,0:T(4,128)}, ...), branch_computations={%region_13.13_spmd, %region_14.14_spmd} | conditional | flops 675282944 | bytes 16203828 | solution.py:179
  290.7 5.6 %conditional.6 = (f32[256,2,4,128]{3,0,2,1:T(8,128)S(1)}, f32[256,256]{0,1:T(8,128)S(1)}, f32[256,256]{0,1:T(8,128)S(1)}) conditional(s32[]{:T(128)} %convert_element_type.204, () %tuple.120, (pred[256,256]{0,1:T(8,128)(4,1)}, bf16[256,256]{1,0:T(8,128)(2,1)}, bf16[256,2,4,128]{0,3,2,1:T(8,128)(2,1)}, f32[2,4,256]{2,1,0:T(4,128)}, ...), branch_computations={%region_13.13_spmd, %region_14.14_spmd} | conditional | flops 675282944 | bytes 16203828 | solution.py:179
  300.6 3.7 collective-permute-done.3
  317.3 5.6 %conditional.6 = (f32[256,2,4,128]{3,0,2,1:T(8,128)S(1)}, f32[256,256]{0,1:T(8,128)S(1)}, f32[256,256]{0,1:T(8,128)S(1)}) conditional(s32[]{:T(128)} %convert_element_type.204, () %tuple.120, (pred[256,256]{0,1:T(8,128)(4,1)}, bf16[256,256]{1,0:T(8,128)(2,1)}, bf16[256,2,4,128]{0,3,2,1:T(8,128)(2,1)}, f32[2,4,256]{2,1,0:T(4,128)}, ...), branch_computations={%region_13.13_spmd, %region_14.14_spmd} | conditional | flops 675282944 | bytes 16203828 | solution.py:179
  324.5 7.5 %collective-permute-done.3 = bf16[256,256]{0,1:T(8,128)(2,1)S(1)} collective-permute-done((bf16[256,256]{0,1:T(8,128)(2,1)S(1)}, bf16[256,256]{0,1:T(8,128)(2,1)S(1)}, u32[]{:S(2)}, u32[]{:S(2)}) %collective-permute-start.3) | collective-permute-done | bytes 131104 | tf_op jit(solution)/shard_map/while/body/eval_jaxpr/ppermute | solution.py:15
  342.9 5.6 %conditional.6 = (f32[256,2,4,128]{3,0,2,1:T(8,128)S(1)}, f32[256,256]{0,1:T(8,128)S(1)}, f32[256,256]{0,1:T(8,128)S(1)}) conditional(s32[]{:T(128)} %convert_element_type.204, () %tuple.120, (pred[256,256]{0,1:T(8,128)(4,1)}, bf16[256,256]{1,0:T(8,128)(2,1)}, bf16[256,2,4,128]{0,3,2,1:T(8,128)(2,1)}, f32[2,4,256]{2,1,0:T(4,128)}, ...), branch_computations={%region_13.13_spmd, %region_14.14_spmd} | conditional | flops 675282944 | bytes 16203828 | solution.py:179
  351.3 5.0 collective-permute-done.3
  366.4 5.6 %conditional.6 = (f32[256,2,4,128]{3,0,2,1:T(8,128)S(1)}, f32[256,256]{0,1:T(8,128)S(1)}, f32[256,256]{0,1:T(8,128)S(1)}) conditional(s32[]{:T(128)} %convert_element_type.204, () %tuple.120, (pred[256,256]{0,1:T(8,128)(4,1)}, bf16[256,256]{1,0:T(8,128)(2,1)}, bf16[256,2,4,128]{0,3,2,1:T(8,128)(2,1)}, f32[2,4,256]{2,1,0:T(4,128)}, ...), branch_computations={%region_13.13_spmd, %region_14.14_spmd} | conditional | flops 675282944 | bytes 16203828 | solution.py:179
  374.2 3.5 collective-permute-start.2
  386.6 3.3 collective-permute-start.1
  394.1 5.6 %conditional.6 = (f32[256,2,4,128]{3,0,2,1:T(8,128)S(1)}, f32[256,256]{0,1:T(8,128)S(1)}, f32[256,256]{0,1:T(8,128)S(1)}) conditional(s32[]{:T(128)} %convert_element_type.204, () %tuple.120, (pred[256,256]{0,1:T(8,128)(4,1)}, bf16[256,256]{1,0:T(8,128)(2,1)}, bf16[256,2,4,128]{0,3,2,1:T(8,128)(2,1)}, f32[2,4,256]{2,1,0:T(4,128)}, ...), branch_computations={%region_13.13_spmd, %region_14.14_spmd} | conditional | flops 675282944 | bytes 16203828 | solution.py:179
  402.7 5.5 %collective-permute-done.3 = bf16[256,256]{0,1:T(8,128)(2,1)S(1)} collective-permute-done((bf16[256,256]{0,1:T(8,128)(2,1)S(1)}, bf16[256,256]{0,1:T(8,128)(2,1)S(1)}, u32[]{:S(2)}, u32[]{:S(2)}) %collective-permute-start.3) | collective-permute-done | bytes 131104 | tf_op jit(solution)/shard_map/while/body/eval_jaxpr/ppermute | solution.py:15
  411.6 3.4 all-to-all-start.5
  417.2 6.0 %all-to-all-done.5 = bf16[8,64,256]{2,1,0:T(8,128)(2,1)S(1)} async-done(((bf16[8,64,256]{2,1,0:T(8,128)(2,1)}), bf16[8,64,256]{2,1,0:T(8,128)(2,1)S(1)}, u32[]{:S(2)}, u32[]{:S(2)}) %all-to-all-start.5) | async-done | bytes 262176 | tf_op jit(solution)/shard_map/all_to_all | solution.py:256
  423.2 3.6 all-to-all-start.4
  429.9 8.7 %all-to-all-done.4 = bf16[8,64,256]{2,1,0:T(8,128)(2,1)S(1)} async-done(((bf16[8,64,256]{2,1,0:T(8,128)(2,1)}), bf16[8,64,256]{2,1,0:T(8,128)(2,1)S(1)}, u32[]{:S(2)}, u32[]{:S(2)}) %all-to-all-start.4) | async-done | bytes 262176 | tf_op jit(solution)/shard_map/all_to_all | solution.py:253
  438.7 3.6 all-to-all-start.3
  442.9 15.6 %all-to-all-done.3 = bf16[8,64,1024]{2,1,0:T(8,128)(2,1)S(1)} async-done(((bf16[8,64,1024]{2,1,0:T(8,128)(2,1)}), bf16[8,64,1024]{2,1,0:T(8,128)(2,1)S(1)}, u32[]{:S(2)}, u32[]{:S(2)}) %all-to-all-start.3) | async-done | bytes 1048608 | tf_op jit(solution)/shard_map/all_to_all | solution.py:250
  459.5 18.9 %fusion.56 = f32[256,8192]{1,0:T(8,128)} fusion(bf16[256,1024]{1,0:T(8,128)(2,1)S(1)} %bitcast.128, bf16[8192,1024]{1,0:T(8,128)(2,1)} %param.16), kind=kOutput, calls=%fused_computation.99 | convolution fusion | flops 4294967296 | bytes 25690112 | tf_op jit(solution)/shard_map/dot_general | solution.py:43
  478.4 6.1 %convolution_add_fusion.1 = f32[256,8192]{1,0:T(8,128)S(1)} fusion(f32[256,8192]{1,0:T(8,128)} %fusion.56, bf16[256,256]{1,0:T(8,128)(2,1)S(1)} %bitcast.133, bf16[8192,256]{1,0:T(8,128)(2,1)} %param.17), kind=kOutput, calls=%fused_computation.39 | convolution fusion | flops 1075838976 | bytes 21102592 | tf_op jit(solution)/shard_map/dot_general | solution.py:43
  484.5 3.3 fusion.24
  490.4 39.7 %reduce-scatter.2.cloned.1.call-done = bf16[256,2048]{1,0:T(8,128)(2,1)} async-done(((bf16[256,8192]{1,0:T(8,128)(2,1)}), bf16[256,2048]{1,0:T(8,128)(2,1)}) %reduce-scatter.2.cloned.1.call-update) | async-done | bytes 1048592 | tf_op jit(solution)/shard_map/reduce_scatter | solution.py:275
  (372 shorter events, 243.1 us)
Async XLA Ops:
  7.2 39.6 %all-gather.3.cloned.1.call-start = ((), (), s32[]{:S(2)}) async-start(), calls=%async_computation.7 | async-start | bytes 5242880 | tf_op jit(solution)/shard_map/all_gather | solution.py:62
  52.6 14.8 %all-to-all-start.2 = ((bf16[8,64,256]{2,1,0:T(8,128)(2,1)}), bf16[8,64,256]{2,1,0:T(8,128)(2,1)S(1)}, u32[]{:S(2)}, u32[]{:S(2)}) async-start(bf16[8,64,256]{2,1,0:T(8,128)(2,1)} %copy.133), calls=%async_computation.2 | async-start | bytes 524288 | tf_op jit(solution)/shard_map/all_to_all | solution.py:83
  67.4 17.4 %all-to-all-start = ((bf16[8,64,256]{2,1,0:T(8,128)(2,1)}), bf16[8,64,256]{2,1,0:T(8,128)(2,1)S(1)}, u32[]{:S(2)}, u32[]{:S(2)}) async-start(bf16[8,64,256]{2,1,0:T(8,128)(2,1)} %copy.117), calls=%async_computation | async-start | bytes 524288 | tf_op jit(solution)/shard_map/all_to_all | solution.py:80
  84.8 60.8 %all-to-all-start.1 = ((bf16[8,64,1024]{2,1,0:T(8,128)(2,1)}), bf16[8,64,1024]{2,1,0:T(8,128)(2,1)}, u32[]{:S(2)}, u32[]{:S(2)}) async-start(bf16[8,64,1024]{2,1,0:T(8,128)(2,1)} %copy.129), calls=%async_computation.1 | async-start | bytes 2097152 | tf_op jit(solution)/shard_map/all_to_all | solution.py:77
  90.8 60.8 %all-gather.5.cloned.1.call-start = ((), (), s32[]{:S(2)}) async-start(), calls=%async_computation.8 | async-start | bytes 1179648 | tf_op jit(solution)/shard_map/all_gather | solution.py:205
  93.7 25.5 %collective-permute-start.4 = (bf16[256,256]{1,0:T(8,128)(2,1)}, bf16[256,256]{1,0:T(8,128)(2,1)S(1)}, u32[]{:S(2)}, u32[]{:S(2)}) collective-permute-start(bf16[256,256]{1,0:T(8,128)(2,1)} %bitcast.26), channel_id=1, source_target_pairs={{0,4},{4,8},{8,12},{12,16},{16,20},{20,24},{24,28},{28,0},{1,5},{5... | collective-permute-start | bytes 393224 | tf_op jit(solution)/shard_map/ppermute | solution.py:196
  100.9 18.6 %collective-permute-start.5 = (bf16[256,256]{1,0:T(8,128)(2,1)}, bf16[256,256]{1,0:T(8,128)(2,1)S(1)}, u32[]{:S(2)}, u32[]{:S(2)}) collective-permute-start(bf16[256,256]{1,0:T(8,128)(2,1)} %bitcast.26), channel_id=1, source_target_pairs={{0,28},{4,0},{8,4},{12,8},{16,12},{20,16},{24,20},{28,24},{1,29},{... | collective-permute-start | bytes 393224 | tf_op jit(solution)/shard_map/ppermute | solution.py:201
  119.4 7.7 %collective-permute-start.6 = (bf16[256,256]{1,0:T(8,128)(2,1)S(1)}, bf16[256,256]{1,0:T(8,128)(2,1)S(1)}, u32[]{:S(2)}, u32[]{:S(2)}) collective-permute-start(bf16[256,256]{1,0:T(8,128)(2,1)S(1)} %collective-permute-done.4), channel_id=1, source_target_pairs={{0,4},{4,8},{8,12},{12,16},{16,20},{20,24},{24,28},{28,0},{1,5},{5... | collective-permute-start | bytes 393224 | tf_op jit(solution)/shard_map/ppermute | solution.py:196
  119.6 9.6 %collective-permute-start.7 = (bf16[256,256]{1,0:T(8,128)(2,1)S(1)}, bf16[256,256]{1,0:T(8,128)(2,1)S(1)}, u32[]{:S(2)}, u32[]{:S(2)}) collective-permute-start(bf16[256,256]{1,0:T(8,128)(2,1)S(1)} %collective-permute-done.5), channel_id=1, source_target_pairs={{0,28},{4,0},{8,4},{12,8},{16,12},{20,16},{24,20},{28,24},{1,29},{... | collective-permute-start | bytes 393224 | tf_op jit(solution)/shard_map/ppermute | solution.py:201
  127.2 8.6 %collective-permute-start.8 = (bf16[256,256]{1,0:T(8,128)(2,1)S(1)}, bf16[256,256]{1,0:T(8,128)(2,1)S(1)}, u32[]{:S(2)}, u32[]{:S(2)}) collective-permute-start(bf16[256,256]{1,0:T(8,128)(2,1)S(1)} %collective-permute-done.6), channel_id=1, source_target_pairs={{0,4},{4,8},{8,12},{12,16},{16,20},{20,24},{24,28},{28,0},{1,5},{5... | collective-permute-start | bytes 393224 | tf_op jit(solution)/shard_map/ppermute | solution.py:196
  129.2 10.9 %collective-permute-start.9 = (bf16[256,256]{1,0:T(8,128)(2,1)S(1)}, bf16[256,256]{1,0:T(8,128)(2,1)S(1)}, u32[]{:S(2)}, u32[]{:S(2)}) collective-permute-start(bf16[256,256]{1,0:T(8,128)(2,1)S(1)} %collective-permute-done.7), channel_id=1, source_target_pairs={{0,28},{4,0},{8,4},{12,8},{16,12},{20,16},{24,20},{28,24},{1,29},{... | collective-permute-start | bytes 393224 | tf_op jit(solution)/shard_map/ppermute | solution.py:201
  135.9 9.5 %collective-permute-start.10 = (bf16[256,256]{1,0:T(8,128)(2,1)S(1)}, bf16[256,256]{1,0:T(8,128)(2,1)S(1)}, u32[]{:S(2)}, u32[]{:S(2)}) collective-permute-start(bf16[256,256]{1,0:T(8,128)(2,1)S(1)} %collective-permute-done.8), channel_id=1, source_target_pairs={{0,4},{4,8},{8,12},{12,16},{16,20},{20,24},{24,28},{28,0},{1,5},{5... | collective-permute-start | bytes 393224 | tf_op jit(solution)/shard_map/ppermute | solution.py:196
  208.6 24.2 %collective-permute-start = (bf16[256,256]{1,0:T(8,128)(2,1)}, bf16[256,256]{1,0:T(8,128)(2,1)}, u32[]{:S(2)}, u32[]{:S(2)}) collective-permute-start(bf16[256,256]{1,0:T(8,128)(2,1)} %copy.256), channel_id=1, source_target_pairs={{0,4},{4,8},{8,12},{12,16},{16,20},{20,24},{24,28},{28,0},{1,5},{5... | collective-permute-start | bytes 393224 | tf_op jit(solution)/shard_map/while/body/eval_jaxpr/ppermute | solution.py:15
  210.2 22.6 %collective-permute-start.1 = (bf16[256,256]{1,0:T(8,128)(2,1)}, bf16[256,256]{1,0:T(8,128)(2,1)}, u32[]{:S(2)}, u32[]{:S(2)}) collective-permute-start(bf16[256,256]{1,0:T(8,128)(2,1)} %copy.257), channel_id=1, source_target_pairs={{0,4},{4,8},{8,12},{12,16},{16,20},{20,24},{24,28},{28,0},{1,5},{5... | collective-permute-start | bytes 393224 | tf_op jit(solution)/shard_map/while/body/eval_jaxpr/ppermute | solution.py:15
  222.9 7.7 %collective-permute-start.3 = (bf16[256,256]{0,1:T(8,128)(2,1)S(1)}, bf16[256,256]{0,1:T(8,128)(2,1)S(1)}, u32[]{:S(2)}, u32[]{:S(2)}) collective-permute-start(bf16[256,256]{0,1:T(8,128)(2,1)S(1)} %fusion.85), channel_id=1, source_target_pairs={{0,4},{4,8},{8,12},{12,16},{16,20},{20,24},{24,28},{28,0},{1,5},{5... | collective-permute-start | bytes 393224 | tf_op jit(solution)/shard_map/while/body/eval_jaxpr/ppermute | solution.py:15
  223.2 8.8 %collective-permute-start.2 = (bf16[256,256]{0,1:T(8,128)(2,1)S(1)}, bf16[256,256]{0,1:T(8,128)(2,1)S(1)}, u32[]{:S(2)}, u32[]{:S(2)}) collective-permute-start(bf16[256,256]{0,1:T(8,128)(2,1)S(1)} %fusion.84), channel_id=1, source_target_pairs={{0,4},{4,8},{8,12},{12,16},{16,20},{20,24},{24,28},{28,0},{1,5},{5... | collective-permute-start | bytes 393224 | tf_op jit(solution)/shard_map/while/body/eval_jaxpr/ppermute | solution.py:15
  234.3 21.7 %collective-permute-start = (bf16[256,256]{1,0:T(8,128)(2,1)}, bf16[256,256]{1,0:T(8,128)(2,1)}, u32[]{:S(2)}, u32[]{:S(2)}) collective-permute-start(bf16[256,256]{1,0:T(8,128)(2,1)} %copy.256), channel_id=1, source_target_pairs={{0,4},{4,8},{8,12},{12,16},{16,20},{20,24},{24,28},{28,0},{1,5},{5... | collective-permute-start | bytes 393224 | tf_op jit(solution)/shard_map/while/body/eval_jaxpr/ppermute | solution.py:15
  235.9 20.2 %collective-permute-start.1 = (bf16[256,256]{1,0:T(8,128)(2,1)}, bf16[256,256]{1,0:T(8,128)(2,1)}, u32[]{:S(2)}, u32[]{:S(2)}) collective-permute-start(bf16[256,256]{1,0:T(8,128)(2,1)} %copy.257), channel_id=1, source_target_pairs={{0,4},{4,8},{8,12},{12,16},{16,20},{20,24},{24,28},{28,0},{1,5},{5... | collective-permute-start | bytes 393224 | tf_op jit(solution)/shard_map/while/body/eval_jaxpr/ppermute | solution.py:15
  246.2 7.7 %collective-permute-start.3 = (bf16[256,256]{0,1:T(8,128)(2,1)S(1)}, bf16[256,256]{0,1:T(8,128)(2,1)S(1)}, u32[]{:S(2)}, u32[]{:S(2)}) collective-permute-start(bf16[256,256]{0,1:T(8,128)(2,1)S(1)} %fusion.85), channel_id=1, source_target_pairs={{0,4},{4,8},{8,12},{12,16},{16,20},{20,24},{24,28},{28,0},{1,5},{5... | collective-permute-start | bytes 393224 | tf_op jit(solution)/shard_map/while/body/eval_jaxpr/ppermute | solution.py:15
  247.3 8.1 %collective-permute-start.2 = (bf16[256,256]{0,1:T(8,128)(2,1)S(1)}, bf16[256,256]{0,1:T(8,128)(2,1)S(1)}, u32[]{:S(2)}, u32[]{:S(2)}) collective-permute-start(bf16[256,256]{0,1:T(8,128)(2,1)S(1)} %fusion.84), channel_id=1, source_target_pairs={{0,4},{4,8},{8,12},{12,16},{16,20},{20,24},{24,28},{28,0},{1,5},{5... | collective-permute-start | bytes 393224 | tf_op jit(solution)/shard_map/while/body/eval_jaxpr/ppermute | solution.py:15
  257.7 23.3 %collective-permute-start = (bf16[256,256]{1,0:T(8,128)(2,1)}, bf16[256,256]{1,0:T(8,128)(2,1)}, u32[]{:S(2)}, u32[]{:S(2)}) collective-permute-start(bf16[256,256]{1,0:T(8,128)(2,1)} %copy.256), channel_id=1, source_target_pairs={{0,4},{4,8},{8,12},{12,16},{16,20},{20,24},{24,28},{28,0},{1,5},{5... | collective-permute-start | bytes 393224 | tf_op jit(solution)/shard_map/while/body/eval_jaxpr/ppermute | solution.py:15
  259.2 21.8 %collective-permute-start.1 = (bf16[256,256]{1,0:T(8,128)(2,1)}, bf16[256,256]{1,0:T(8,128)(2,1)}, u32[]{:S(2)}, u32[]{:S(2)}) collective-permute-start(bf16[256,256]{1,0:T(8,128)(2,1)} %copy.257), channel_id=1, source_target_pairs={{0,4},{4,8},{8,12},{12,16},{16,20},{20,24},{24,28},{28,0},{1,5},{5... | collective-permute-start | bytes 393224 | tf_op jit(solution)/shard_map/while/body/eval_jaxpr/ppermute | solution.py:15
  270.2 7.7 %collective-permute-start.3 = (bf16[256,256]{0,1:T(8,128)(2,1)S(1)}, bf16[256,256]{0,1:T(8,128)(2,1)S(1)}, u32[]{:S(2)}, u32[]{:S(2)}) collective-permute-start(bf16[256,256]{0,1:T(8,128)(2,1)S(1)} %fusion.85), channel_id=1, source_target_pairs={{0,4},{4,8},{8,12},{12,16},{16,20},{20,24},{24,28},{28,0},{1,5},{5... | collective-permute-start | bytes 393224 | tf_op jit(solution)/shard_map/while/body/eval_jaxpr/ppermute | solution.py:15
  272.5 7.7 %collective-permute-start.2 = (bf16[256,256]{0,1:T(8,128)(2,1)S(1)}, bf16[256,256]{0,1:T(8,128)(2,1)S(1)}, u32[]{:S(2)}, u32[]{:S(2)}) collective-permute-start(bf16[256,256]{0,1:T(8,128)(2,1)S(1)} %fusion.84), channel_id=1, source_target_pairs={{0,4},{4,8},{8,12},{12,16},{16,20},{20,24},{24,28},{28,0},{1,5},{5... | collective-permute-start | bytes 393224 | tf_op jit(solution)/shard_map/while/body/eval_jaxpr/ppermute | solution.py:15
  282.6 25.4 %collective-permute-start = (bf16[256,256]{1,0:T(8,128)(2,1)}, bf16[256,256]{1,0:T(8,128)(2,1)}, u32[]{:S(2)}, u32[]{:S(2)}) collective-permute-start(bf16[256,256]{1,0:T(8,128)(2,1)} %copy.256), channel_id=1, source_target_pairs={{0,4},{4,8},{8,12},{12,16},{16,20},{20,24},{24,28},{28,0},{1,5},{5... | collective-permute-start | bytes 393224 | tf_op jit(solution)/shard_map/while/body/eval_jaxpr/ppermute | solution.py:15
  284.9 23.1 %collective-permute-start.1 = (bf16[256,256]{1,0:T(8,128)(2,1)}, bf16[256,256]{1,0:T(8,128)(2,1)}, u32[]{:S(2)}, u32[]{:S(2)}) collective-permute-start(bf16[256,256]{1,0:T(8,128)(2,1)} %copy.257), channel_id=1, source_target_pairs={{0,4},{4,8},{8,12},{12,16},{16,20},{20,24},{24,28},{28,0},{1,5},{5... | collective-permute-start | bytes 393224 | tf_op jit(solution)/shard_map/while/body/eval_jaxpr/ppermute | solution.py:15
  296.3 8.0 %collective-permute-start.3 = (bf16[256,256]{0,1:T(8,128)(2,1)S(1)}, bf16[256,256]{0,1:T(8,128)(2,1)S(1)}, u32[]{:S(2)}, u32[]{:S(2)}) collective-permute-start(bf16[256,256]{0,1:T(8,128)(2,1)S(1)} %fusion.85), channel_id=1, source_target_pairs={{0,4},{4,8},{8,12},{12,16},{16,20},{20,24},{24,28},{28,0},{1,5},{5... | collective-permute-start | bytes 393224 | tf_op jit(solution)/shard_map/while/body/eval_jaxpr/ppermute | solution.py:15
  298.2 9.1 %collective-permute-start.2 = (bf16[256,256]{0,1:T(8,128)(2,1)S(1)}, bf16[256,256]{0,1:T(8,128)(2,1)S(1)}, u32[]{:S(2)}, u32[]{:S(2)}) collective-permute-start(bf16[256,256]{0,1:T(8,128)(2,1)S(1)} %fusion.84), channel_id=1, source_target_pairs={{0,4},{4,8},{8,12},{12,16},{16,20},{20,24},{24,28},{28,0},{1,5},{5... | collective-permute-start | bytes 393224 | tf_op jit(solution)/shard_map/while/body/eval_jaxpr/ppermute | solution.py:15
  309.6 26.0 %collective-permute-start = (bf16[256,256]{1,0:T(8,128)(2,1)}, bf16[256,256]{1,0:T(8,128)(2,1)}, u32[]{:S(2)}, u32[]{:S(2)}) collective-permute-start(bf16[256,256]{1,0:T(8,128)(2,1)} %copy.256), channel_id=1, source_target_pairs={{0,4},{4,8},{8,12},{12,16},{16,20},{20,24},{24,28},{28,0},{1,5},{5... | collective-permute-start | bytes 393224 | tf_op jit(solution)/shard_map/while/body/eval_jaxpr/ppermute | solution.py:15
  311.1 24.5 %collective-permute-start.1 = (bf16[256,256]{1,0:T(8,128)(2,1)}, bf16[256,256]{1,0:T(8,128)(2,1)}, u32[]{:S(2)}, u32[]{:S(2)}) collective-permute-start(bf16[256,256]{1,0:T(8,128)(2,1)} %copy.257), channel_id=1, source_target_pairs={{0,4},{4,8},{8,12},{12,16},{16,20},{20,24},{24,28},{28,0},{1,5},{5... | collective-permute-start | bytes 393224 | tf_op jit(solution)/shard_map/while/body/eval_jaxpr/ppermute | solution.py:15
  323.0 9.1 %collective-permute-start.3 = (bf16[256,256]{0,1:T(8,128)(2,1)S(1)}, bf16[256,256]{0,1:T(8,128)(2,1)S(1)}, u32[]{:S(2)}, u32[]{:S(2)}) collective-permute-start(bf16[256,256]{0,1:T(8,128)(2,1)S(1)} %fusion.85), channel_id=1, source_target_pairs={{0,4},{4,8},{8,12},{12,16},{16,20},{20,24},{24,28},{28,0},{1,5},{5... | collective-permute-start | bytes 393224 | tf_op jit(solution)/shard_map/while/body/eval_jaxpr/ppermute | solution.py:15
  324.1 10.7 %collective-permute-start.2 = (bf16[256,256]{0,1:T(8,128)(2,1)S(1)}, bf16[256,256]{0,1:T(8,128)(2,1)S(1)}, u32[]{:S(2)}, u32[]{:S(2)}) collective-permute-start(bf16[256,256]{0,1:T(8,128)(2,1)S(1)} %fusion.84), channel_id=1, source_target_pairs={{0,4},{4,8},{8,12},{12,16},{16,20},{20,24},{24,28},{28,0},{1,5},{5... | collective-permute-start | bytes 393224 | tf_op jit(solution)/shard_map/while/body/eval_jaxpr/ppermute | solution.py:15
  337.2 21.2 %collective-permute-start = (bf16[256,256]{1,0:T(8,128)(2,1)}, bf16[256,256]{1,0:T(8,128)(2,1)}, u32[]{:S(2)}, u32[]{:S(2)}) collective-permute-start(bf16[256,256]{1,0:T(8,128)(2,1)} %copy.256), channel_id=1, source_target_pairs={{0,4},{4,8},{8,12},{12,16},{16,20},{20,24},{24,28},{28,0},{1,5},{5... | collective-permute-start | bytes 393224 | tf_op jit(solution)/shard_map/while/body/eval_jaxpr/ppermute | solution.py:15
  338.7 19.7 %collective-permute-start.1 = (bf16[256,256]{1,0:T(8,128)(2,1)}, bf16[256,256]{1,0:T(8,128)(2,1)}, u32[]{:S(2)}, u32[]{:S(2)}) collective-permute-start(bf16[256,256]{1,0:T(8,128)(2,1)} %copy.257), channel_id=1, source_target_pairs={{0,4},{4,8},{8,12},{12,16},{16,20},{20,24},{24,28},{28,0},{1,5},{5... | collective-permute-start | bytes 393224 | tf_op jit(solution)/shard_map/while/body/eval_jaxpr/ppermute | solution.py:15
  348.5 7.7 %collective-permute-start.3 = (bf16[256,256]{0,1:T(8,128)(2,1)S(1)}, bf16[256,256]{0,1:T(8,128)(2,1)S(1)}, u32[]{:S(2)}, u32[]{:S(2)}) collective-permute-start(bf16[256,256]{0,1:T(8,128)(2,1)S(1)} %fusion.85), channel_id=1, source_target_pairs={{0,4},{4,8},{8,12},{12,16},{16,20},{20,24},{24,28},{28,0},{1,5},{5... | collective-permute-start | bytes 393224 | tf_op jit(solution)/shard_map/while/body/eval_jaxpr/ppermute | solution.py:15
  349.6 8.1 %collective-permute-start.2 = (bf16[256,256]{0,1:T(8,128)(2,1)S(1)}, bf16[256,256]{0,1:T(8,128)(2,1)S(1)}, u32[]{:S(2)}, u32[]{:S(2)}) collective-permute-start(bf16[256,256]{0,1:T(8,128)(2,1)S(1)} %fusion.84), channel_id=1, source_target_pairs={{0,4},{4,8},{8,12},{12,16},{16,20},{20,24},{24,28},{28,0},{1,5},{5... | collective-permute-start | bytes 393224 | tf_op jit(solution)/shard_map/while/body/eval_jaxpr/ppermute | solution.py:15
  360.0 22.7 %collective-permute-start = (bf16[256,256]{1,0:T(8,128)(2,1)}, bf16[256,256]{1,0:T(8,128)(2,1)}, u32[]{:S(2)}, u32[]{:S(2)}) collective-permute-start(bf16[256,256]{1,0:T(8,128)(2,1)} %copy.256), channel_id=1, source_target_pairs={{0,4},{4,8},{8,12},{12,16},{16,20},{20,24},{24,28},{28,0},{1,5},{5... | collective-permute-start | bytes 393224 | tf_op jit(solution)/shard_map/while/body/eval_jaxpr/ppermute | solution.py:15
  361.5 21.1 %collective-permute-start.1 = (bf16[256,256]{1,0:T(8,128)(2,1)}, bf16[256,256]{1,0:T(8,128)(2,1)}, u32[]{:S(2)}, u32[]{:S(2)}) collective-permute-start(bf16[256,256]{1,0:T(8,128)(2,1)} %copy.257), channel_id=1, source_target_pairs={{0,4},{4,8},{8,12},{12,16},{16,20},{20,24},{24,28},{28,0},{1,5},{5... | collective-permute-start | bytes 393224 | tf_op jit(solution)/shard_map/while/body/eval_jaxpr/ppermute | solution.py:15
  372.1 7.7 %collective-permute-start.3 = (bf16[256,256]{0,1:T(8,128)(2,1)S(1)}, bf16[256,256]{0,1:T(8,128)(2,1)S(1)}, u32[]{:S(2)}, u32[]{:S(2)}) collective-permute-start(bf16[256,256]{0,1:T(8,128)(2,1)S(1)} %fusion.85), channel_id=1, source_target_pairs={{0,4},{4,8},{8,12},{12,16},{16,20},{20,24},{24,28},{28,0},{1,5},{5... | collective-permute-start | bytes 393224 | tf_op jit(solution)/shard_map/while/body/eval_jaxpr/ppermute | solution.py:15
  374.2 7.7 %collective-permute-start.2 = (bf16[256,256]{0,1:T(8,128)(2,1)S(1)}, bf16[256,256]{0,1:T(8,128)(2,1)S(1)}, u32[]{:S(2)}, u32[]{:S(2)}) collective-permute-start(bf16[256,256]{0,1:T(8,128)(2,1)S(1)} %fusion.84), channel_id=1, source_target_pairs={{0,4},{4,8},{8,12},{12,16},{16,20},{20,24},{24,28},{28,0},{1,5},{5... | collective-permute-start | bytes 393224 | tf_op jit(solution)/shard_map/while/body/eval_jaxpr/ppermute | solution.py:15
  384.2 26.2 %collective-permute-start = (bf16[256,256]{1,0:T(8,128)(2,1)}, bf16[256,256]{1,0:T(8,128)(2,1)}, u32[]{:S(2)}, u32[]{:S(2)}) collective-permute-start(bf16[256,256]{1,0:T(8,128)(2,1)} %copy.256), channel_id=1, source_target_pairs={{0,4},{4,8},{8,12},{12,16},{16,20},{20,24},{24,28},{28,0},{1,5},{5... | collective-permute-start | bytes 393224 | tf_op jit(solution)/shard_map/while/body/eval_jaxpr/ppermute | solution.py:15
  386.6 23.9 %collective-permute-start.1 = (bf16[256,256]{1,0:T(8,128)(2,1)}, bf16[256,256]{1,0:T(8,128)(2,1)}, u32[]{:S(2)}, u32[]{:S(2)}) collective-permute-start(bf16[256,256]{1,0:T(8,128)(2,1)} %copy.257), channel_id=1, source_target_pairs={{0,4},{4,8},{8,12},{12,16},{16,20},{20,24},{24,28},{28,0},{1,5},{5... | collective-permute-start | bytes 393224 | tf_op jit(solution)/shard_map/while/body/eval_jaxpr/ppermute | solution.py:15
  399.7 8.6 %collective-permute-start.3 = (bf16[256,256]{0,1:T(8,128)(2,1)S(1)}, bf16[256,256]{0,1:T(8,128)(2,1)S(1)}, u32[]{:S(2)}, u32[]{:S(2)}) collective-permute-start(bf16[256,256]{0,1:T(8,128)(2,1)S(1)} %fusion.85), channel_id=1, source_target_pairs={{0,4},{4,8},{8,12},{12,16},{16,20},{20,24},{24,28},{28,0},{1,5},{5... | collective-permute-start | bytes 393224 | tf_op jit(solution)/shard_map/while/body/eval_jaxpr/ppermute | solution.py:15
  401.1 8.6 %collective-permute-start.2 = (bf16[256,256]{0,1:T(8,128)(2,1)S(1)}, bf16[256,256]{0,1:T(8,128)(2,1)S(1)}, u32[]{:S(2)}, u32[]{:S(2)}) collective-permute-start(bf16[256,256]{0,1:T(8,128)(2,1)S(1)} %fusion.84), channel_id=1, source_target_pairs={{0,4},{4,8},{8,12},{12,16},{16,20},{20,24},{24,28},{28,0},{1,5},{5... | collective-permute-start | bytes 393224 | tf_op jit(solution)/shard_map/while/body/eval_jaxpr/ppermute | solution.py:15
  411.6 11.6 %all-to-all-start.5 = ((bf16[8,64,256]{2,1,0:T(8,128)(2,1)}), bf16[8,64,256]{2,1,0:T(8,128)(2,1)S(1)}, u32[]{:S(2)}, u32[]{:S(2)}) async-start(bf16[8,64,256]{2,1,0:T(8,128)(2,1)} %copy.153), calls=%async_computation.5 | async-start | bytes 524288 | tf_op jit(solution)/shard_map/all_to_all | solution.py:256
  423.2 15.4 %all-to-all-start.4 = ((bf16[8,64,256]{2,1,0:T(8,128)(2,1)}), bf16[8,64,256]{2,1,0:T(8,128)(2,1)S(1)}, u32[]{:S(2)}, u32[]{:S(2)}) async-start(bf16[8,64,256]{2,1,0:T(8,128)(2,1)} %copy.148), calls=%async_computation.4 | async-start | bytes 524288 | tf_op jit(solution)/shard_map/all_to_all | solution.py:253
  438.7 19.9 %all-to-all-start.3 = ((bf16[8,64,1024]{2,1,0:T(8,128)(2,1)}), bf16[8,64,1024]{2,1,0:T(8,128)(2,1)S(1)}, u32[]{:S(2)}, u32[]{:S(2)}) async-start(bf16[8,64,1024]{2,1,0:T(8,128)(2,1)} %copy.143), calls=%async_computation.3 | async-start | bytes 2097152 | tf_op jit(solution)/shard_map/all_to_all | solution.py:250
  442.2 87.9 %reduce-scatter.2.cloned.1.call-start = ((), (), s32[]{:S(2)}) async-start(), calls=%async_computation.9 | async-start | bytes 5242880 | tf_op jit(solution)/shard_map/reduce_scatter | solution.py:275
  (25 other events, 499.8 us)
Sparse Core Ops, SparseCore 0:
  9.6 37.1 all-gather.2
  93.8 55.3 all-gather.4
  487.9 42.1 reduce-scatter.1
